TPU v7x, 256 devices: a whole 4x4x8 slice. The times are simulated.
256 devices in a mesh: shard: 32 (over z, x), tensor: 4 (over y), section: 2 (over core).
Axes of the slice: x: 4, y: 4, z: 8, core: 2. Of those that a mesh axis runs over, the one named last changes fastest.
Arguments:
- grad_parts: bfloat16 [8, 32, 1024, 1024], P(('tensor', 'section'), None, 'shard')
- weights: bfloat16 [32, 1024, 1024], P(None, 'shard', ('tensor', 'section')), may hold values from -6 to 6
- adam_m: float32 [32, 1024, 1024], P(None, 'shard', ('tensor', 'section'))
- adam_v: float32 [32, 1024, 1024], P(None, 'shard', ('tensor', 'section')), may hold values from 0.01 to 1
- left_stat: float32 [96, 1024, 1024], P('shard', None, ('tensor', 'section')), may hold values from -18 to 18
- right_stat: float32 [96, 1024, 1024], P('shard', None, ('tensor', 'section')), may hold values from -18 to 18
- left_root: bfloat16 [32, 1024, 1024], P(None, 'shard', ('tensor', 'section')), as said below
- right_root: bfloat16 [32, 1024, 1024], P(None, 'shard', ('tensor', 'section')), as said below
- block_owner: int32 [32], replicated, may hold values from 0 to 31, as said below
- block_matrix: int32 [32], replicated, may hold values from 0 to 4, as said below
- factors: float32 [832, 2048], P('shard', ('tensor', 'section')), may hold values from -6 to 6
- factor_grad: bfloat16 [832, 2048], P('shard', ('tensor', 'section')), may hold values from -6 to 6
- factor_m: float32 [832, 2048], P('shard', ('tensor', 'section')), may hold values from -3 to 3
- factor_v: float32 [832, 2048], P('shard', ('tensor', 'section')), may hold values from 0.2 to 2
Outputs:
- new_weights: bfloat16 [32, 1024, 1024], P(None, 'shard')
- adam_m_new: float32 [32, 1024, 1024], P(None, 'shard', ('tensor', 'section'))
- adam_v_new: float32 [32, 1024, 1024], P(None, 'shard', ('tensor', 'section'))
- left_new: float32 [96, 1024, 1024], P('shard', None, ('tensor', 'section'))
- right_new: float32 [96, 1024, 1024], P('shard', None, ('tensor', 'section'))
- factors_new: float32 [832, 2048], P('shard', ('tensor', 'section'))
- factor_m_new: float32 [832, 2048], P('shard', ('tensor', 'section'))
- factor_v_new: float32 [832, 2048], P('shard', ('tensor', 'section'))
Inputs may be any that keep to these rules, and one draw needn't show every extreme that they name: `block_owner`: no owner holds more than 3 blocks, and some owner holds exactly 3. `block_matrix`: matrices 0 to 3 hold 4 blocks each, all other blocks belong to matrix 4. `left_root`: every block is symmetric. `right_root`: every block is symmetric.
All inputs are finite; a program needn't handle non-finite values.
Results may differ from a plain program's by a relative error of at most 0.014.
Values may be sent and summed in bfloat16 or wider, within the bound.
A program may use at most 128 MiB of HBM per device.

v0:
```python
import jax
import jax.numpy as jnp
from jax import lax
from jax.sharding import PartitionSpec as P

B = 1024
MATS = 5


BETA_ONE = 0.9
BETA_TWO = 0.95
BETA_STAT = 0.95
LEARNING = 0.1
DECAY_RATE = 0.1
EPSILON = 1e-08
FLOOR_RATE = 1e-06
CORRECT_ONE = 1.0 - 0.9**10
CORRECT_TWO = 1.0 - 0.95**10


def adam_direction(grad_float, moment, second):
    moment_new = BETA_ONE * moment + (1.0 - BETA_ONE) * grad_float
    second_new = BETA_TWO * second + (1.0 - BETA_TWO) * grad_float * grad_float
    direction = moment_new / CORRECT_ONE / (jnp.sqrt(second_new / CORRECT_TWO) + EPSILON)
    return (moment_new, second_new, direction)


def slot_numbers(block_owner, capacity):
    positions = jnp.arange(block_owner.shape[0], dtype=jnp.int32)
    earlier = (block_owner[:, None] == block_owner[None, :]) & (
        positions[None, :] < positions[:, None]
    )
    return block_owner * capacity + jnp.sum(earlier.astype(jnp.int32), axis=1)


def slot_contents(slot, slot_total):
    positions = jnp.arange(slot.shape[0], dtype=jnp.int32)
    matches = jnp.arange(slot_total, dtype=jnp.int32)[:, None] == slot[None, :]
    occupied = jnp.any(matches, axis=1)
    block_ids = jnp.sum(jnp.where(matches, positions[None, :], 0), axis=1)
    return (block_ids, occupied)


def fill_slots(tiles, block_ids, occupied):
    picked = jnp.take(tiles, block_ids, axis=0)
    return jnp.where(occupied[:, None, None], picked, jnp.zeros_like(picked))


def shards(
    grad_parts,
    weights,
    adam_m,
    adam_v,
    left_stat,
    right_stat,
    left_root,
    right_root,
    block_owner,
    block_matrix,
    factors,
    factor_grad,
    factor_m,
    factor_v,
):
    capacity = left_stat.shape[0]
    owners = lax.axis_size("shard")
    owner_index = lax.axis_index("shard")
    group_index = lax.axis_index(("tensor", "section"))
    partials = grad_parts[0].astype(jnp.float32)
    gradient = lax.psum_scatter(
        partials.astype(jnp.bfloat16), ("tensor", "section"), scatter_dimension=2, tiled=True
    )
    gradient = lax.optimization_barrier(gradient)
    grad_float = gradient.astype(jnp.float32)
    adam_m_new, adam_v_new, direction = adam_direction(grad_float, adam_m, adam_v)
    matrix_range = jnp.arange(MATS, dtype=jnp.int32)
    onehot = (block_matrix[:, None] == matrix_range[None, :]).astype(jnp.float32)
    adam_part = jnp.sum(jnp.sum(direction * direction, axis=(1, 2))[:, None] * onehot, axis=0)
    slot = slot_numbers(block_owner, capacity)
    block_ids, occupied = slot_contents(slot, owners * capacity)
    slab_width = gradient.shape[2]
    grad_rows, right_rows = (
        lax.all_gather(gradient, ("tensor", "section"), axis=2, tiled=True),
        lax.all_gather(right_root, ("tensor", "section"), axis=2, tiled=True),
    )
    grad_full, right_full, left_cols = (
        lax.all_to_all(
            fill_slots(grad_rows, block_ids, occupied),
            "shard",
            split_axis=0,
            concat_axis=1,
            tiled=True,
        ),
        lax.all_to_all(
            fill_slots(right_rows, block_ids, occupied),
            "shard",
            split_axis=0,
            concat_axis=1,
            tiled=True,
        ),
        lax.all_to_all(
            fill_slots(left_root, block_ids, occupied),
            "shard",
            split_axis=0,
            concat_axis=1,
            tiled=True,
        ),
    )
    first_row = group_index * slab_width
    grad_rows_own = lax.dynamic_slice_in_dim(grad_full, first_row, slab_width, 1)
    grad_cols_own = lax.dynamic_slice_in_dim(grad_full, first_row, slab_width, 2)
    gram_left = jnp.einsum(
        "sik,sjk->sij", grad_full, grad_rows_own, preferred_element_type=jnp.float32
    )
    gram_right = jnp.einsum(
        "ski,skj->sij", grad_full, grad_cols_own, preferred_element_type=jnp.float32
    )
    left_new = BETA_STAT * left_stat + (1.0 - BETA_STAT) * gram_left
    right_new = BETA_STAT * right_stat + (1.0 - BETA_STAT) * gram_right
    mixed = jnp.einsum(
        "sjc,sjk->sck", left_cols, grad_full, preferred_element_type=jnp.float32
    ).astype(jnp.bfloat16)
    precond = jnp.einsum("sck,skj->scj", mixed, right_full, preferred_element_type=jnp.float32)
    own_blocks = lax.dynamic_slice_in_dim(block_ids, owner_index * capacity, capacity)
    own_occupied = lax.dynamic_slice_in_dim(occupied, owner_index * capacity, capacity)
    own_matrix = jnp.take(block_matrix, own_blocks)
    slot_onehot = ((own_matrix[:, None] == matrix_range[None, :]) & own_occupied[:, None]).astype(
        jnp.float32
    )
    shampoo_part = jnp.sum(jnp.sum(precond * precond, axis=(1, 2))[:, None] * slot_onehot, axis=0)
    adam_norm, shampoo_norm = lax.psum((adam_part, shampoo_part), ("shard", "tensor", "section"))
    precond_half = precond.astype(jnp.bfloat16)
    returned = lax.all_to_all(
        lax.all_to_all(
            precond_half, ("tensor", "section"), split_axis=2, concat_axis=1, tiled=True
        ),
        "shard",
        split_axis=1,
        concat_axis=0,
        tiled=True,
    )
    precond_tile = jnp.take(returned, slot, axis=0).astype(jnp.float32)
    counts = jnp.sum(onehot, axis=0) * float(B * B)
    graft_scale = jnp.sqrt(adam_norm / (shampoo_norm + FLOOR_RATE * counts))
    block_scale = jnp.sum(onehot * graft_scale[None, :], axis=1)
    weights_float = weights.astype(jnp.float32)
    updated = (
        weights_float
        - LEARNING * (block_scale[:, None, None] * precond_tile + DECAY_RATE * weights_float)
    ).astype(jnp.bfloat16)
    factor_m_new, factor_v_new, factor_step = adam_direction(
        factor_grad.astype(jnp.float32), factor_m, factor_v
    )
    factors_new = factors - LEARNING * (factor_step + DECAY_RATE * factors)
    new_weights = lax.all_gather(updated, ("tensor", "section"), axis=2, tiled=True)
    return (
        new_weights,
        adam_m_new,
        adam_v_new,
        left_new,
        right_new,
        factors_new,
        factor_m_new,
        factor_v_new,
    )


def solution(mesh):
    in_specs = (
        P(("tensor", "section"), None, "shard", None),
        P(None, "shard", ("tensor", "section")),
        P(None, "shard", ("tensor", "section")),
        P(None, "shard", ("tensor", "section")),
        P("shard", None, ("tensor", "section")),
        P("shard", None, ("tensor", "section")),
        P(None, "shard", ("tensor", "section")),
        P(None, "shard", ("tensor", "section")),
        P(),
        P(),
        P("shard", ("tensor", "section")),
        P("shard", ("tensor", "section")),
        P("shard", ("tensor", "section")),
        P("shard", ("tensor", "section")),
    )
    out_specs = (
        P(None, "shard", None),
        P(None, "shard", ("tensor", "section")),
        P(None, "shard", ("tensor", "section")),
        P("shard", None, ("tensor", "section")),
        P("shard", None, ("tensor", "section")),
        P("shard", ("tensor", "section")),
        P("shard", ("tensor", "section")),
        P("shard", ("tensor", "section")),
    )
    return jax.shard_map(shards, mesh=mesh, in_specs=in_specs, out_specs=out_specs, check_vma=False)
```

profile of v0, /device:TPU:1, one launch (start us, length us, event | category | flops | bytes accessed | tf_op | source)
XLA Modules:
  0.0 612.7 jit_solution(2450731858968007062)
XLA Ops:
  7.2 12.6 %copy.68 = bf16[32,32,1024]{1,0,2:T(8,128)(2,1)} copy(bf16[32,32,1024]{2,1,0:T(8,128)(2,1)} %bitcast.46) | data formatting | bytes 4194304
  19.8 12.4 %reshape.109 = bf16[1024,1024]{1,0:T(8,128)(2,1)} reshape(bf16[1024,32,32]{2,1,0:T(8,128)(2,1)} %bitcast.37) | data formatting | bytes 4194304
  32.3 0.7 all-gather.6.cloned.1.call-update
  33.0 37.1 %reduce-scatter.4.cloned.1.call-done = bf16[128,1024]{1,0:T(8,128)(2,1)} async-done(((bf16[1024,1024]{1,0:T(8,128)(2,1)}), bf16[128,1024]{1,0:T(8,128)(2,1)}) %reduce-scatter.4.cloned.1.call-update) | async-done | bytes 262160
  70.1 1.8 reshape.110
  72.0 1.8 copy.69
  74.1 0.7 gather_fusion.1
  74.9 1.2 select_select_fusion.2
  76.1 9.2 %all-to-all-start = ((bf16[96,32,128]{2,1,0:T(8,128)(2,1)}), bf16[96,32,128]{2,1,0:T(8,128)(2,1)S(1)}, u32[]{:S(2)}, u32[]{:S(2)}) async-start(bf16[96,32,128]{2,1,0:T(8,128)(2,1)} %select_select_fusion.2), calls=%async_computation | async-start | bytes 1572864 | tf_op jit(solution)/shard_map/all_to_all | solution.py:101
  85.3 17.7 %all-gather.6.cloned.1.call-done = bf16[32,32,1024]{2,1,0:T(8,128)(2,1)} async-done(((bf16[32,32,128]{2,1,0:T(8,128)(2,1)}), bf16[32,32,1024]{2,1,0:T(8,128)(2,1)}) %all-gather.6.cloned.1.call-update) | async-done | bytes 2097168 | tf_op jit(solution)/shard_map/all_gather | solution.py:84
  103.0 7.5 %gather_fusion.4 = bf16[96,32,1024]{2,1,0:T(8,128)(2,1)} fusion(bf16[32,32,1024]{2,1,0:T(8,128)(2,1)} %all-gather.6.cloned.1.call-done, s32[1024]{0:T(1024)S(1)} %pad_clamp_fusion.1), kind=kCustom, calls=%fused_computation.1.clone | custom fusion | bytes 12583296 | tf_op jit(solution)/shard_map/jit(_take)/gather | solution.py:45
  110.5 25.4 %all-gather.4.cloned.1.call-done = bf16[32,32,1024]{2,1,0:T(8,128)(2,1)} async-done(((bf16[32,32,128]{2,1,0:T(8,128)(2,1)}), bf16[32,32,1024]{2,1,0:T(8,128)(2,1)}) %all-gather.4.cloned.1.call-update) | async-done | bytes 2097168 | tf_op jit(solution)/shard_map/all_gather | solution.py:83
  135.9 7.5 %gather_fusion.3 = bf16[96,32,1024]{2,1,0:T(8,128)(2,1)} fusion(bf16[32,32,1024]{2,1,0:T(8,128)(2,1)} %all-gather.4.cloned.1.call-done, s32[1024]{0:T(1024)S(1)} %pad_clamp_fusion.1), kind=kCustom, calls=%fused_computation.clone | custom fusion | bytes 12583296 | tf_op jit(solution)/shard_map/jit(_take)/gather | solution.py:45
  143.4 10.6 %select_select_fusion.1 = (bf16[96,32,1024]{2,1,0:T(8,128)(2,1)}, bf16[96,32,1024]{2,1,0:T(8,128)(2,1)}) fusion(bf16[96,32,1024]{2,1,0:T(8,128)(2,1)} %gather_fusion.3, pred[96]{0:T(512)(128)(4,1)S(1)} %compare_and_fusion.1, pred[96]{0:T(512)(128)(4,1)S(1)} %fusion.10, bf16[96,32,1024]{2,1,0:T(8,128)(2,1)} %gather_fusion.4), kind=kLoop, calls=%fused_computation.6 | loop fusion | flops 12582912 | bytes 25166016 | tf_op jit(solution)/shard_map/jit(_where)/select_n | solution.py:46
  154.0 148.7 %all_to_all.90 = bf16[96,32,1024]{2,1,0:T(8,128)(2,1)} all-to-all(bf16[96,32,1024]{2,1,0:T(8,128)(2,1)} %get-tuple-element.23), channel_id=1, replica_groups=mesh['shard'=32,'tensor'=4,'section'=2] {'shard'}, dimensions={0} | all-to-all | bytes 12582912 | tf_op jit(solution)/shard_map/all_to_all | solution.py:87
  302.8 6.1 all-to-all-start.2
  308.9 6.8 %copy.56 = bf16[32,3,32,1024]{3,2,0,1:T(8,128)(2,1)} copy(bf16[32,3,32,1024]{3,2,1,0:T(8,128)(2,1)} %bitcast.38) | data formatting | bytes 12582912 | tf_op jit(solution)/shard_map/all_to_all | solution.py:87
  315.7 129.0 %all-to-all-done.2 = bf16[96,32,1024]{2,1,0:T(8,128)(2,1)} async-done(((bf16[96,32,1024]{2,1,0:T(8,128)(2,1)}), bf16[96,32,1024]{2,1,0:T(8,128)(2,1)}, u32[]{:S(2)}, u32[]{:S(2)}) %all-to-all-start.2) | async-done | bytes 6291488 | tf_op jit(solution)/shard_map/all_to_all | solution.py:94
  444.7 6.8 %copy.58 = bf16[32,3,32,1024]{3,2,0,1:T(8,128)(2,1)} copy(bf16[32,3,32,1024]{3,2,1,0:T(8,128)(2,1)} %bitcast.9) | data formatting | bytes 12582912 | tf_op jit(solution)/shard_map/all_to_all | solution.py:94
  451.5 6.6 %multiply_reduce_fusion = (f32[3]{0:T(128)S(1)}, bf16[3,128,1024]{2,1,0:T(8,128)(2,1)S(1)}) fusion(bf16[3,1024,1024]{2,1,0:T(8,128)(2,1)} %bitcast.39, bf16[3,1024,128]{2,1,0:T(8,128)(2,1)S(1)} %bitcast.41, bf16[3,1024,1024]{2,1,0:T(8,128)(2,1)} %bitcast.32), kind=kOutput, calls=%fused_computation.9 | convolution fusion | flops 1612185600 | bytes 14155788 | tf_op jit(solution)/shard_map/sck,skj->scj/dot_general | solution.py:123
  458.1 1.4 copy.59
  459.5 10.0 %all-to-all-start.3 = ((bf16[3,128,1024]{1,0,2:T(4,128)(2,1)}), bf16[3,128,1024]{1,0,2:T(4,128)(2,1)S(1)}, u32[]{:S(2)}, u32[]{:S(2)}) async-start(bf16[3,128,1024]{1,0,2:T(4,128)(2,1)} %copy.59), calls=%async_computation.3 | async-start | bytes 2097152 | tf_op jit(solution)/shard_map/all_to_all | solution.py:134
  469.6 15.0 %all-to-all-done.3 = bf16[3,128,1024]{1,0,2:T(4,128)(2,1)S(1)} async-done(((bf16[3,128,1024]{1,0,2:T(4,128)(2,1)}), bf16[3,128,1024]{1,0,2:T(4,128)(2,1)S(1)}, u32[]{:S(2)}, u32[]{:S(2)}) %all-to-all-start.3) | async-done | bytes 786464 | tf_op jit(solution)/shard_map/all_to_all | solution.py:134
  485.1 1.6 copy.62
  486.7 7.5 %all-to-all-start.4 = ((bf16[3,1024,128]{2,0,1:T(4,128)(2,1)}), bf16[3,1024,128]{2,0,1:T(4,128)(2,1)S(1)}, u32[]{:S(2)}, u32[]{:S(2)}) async-start(bf16[3,1024,128]{2,0,1:T(4,128)(2,1)} %copy.62), calls=%async_computation.4 | async-start | bytes 2097152 | tf_op jit(solution)/shard_map/all_to_all | solution.py:133
  495.2 1.4 multiply_reduce_fusion.1
  496.8 77.3 %all-reduce = (f32[5]{0:T(128)S(1)}, f32[5]{0:T(128)S(1)}) all-reduce(f32[5]{0:T(128)S(1)} %get-tuple-element.10, f32[5]{0:T(128)S(1)} %select_reduce_fusion.3), channel_id=1, replica_groups=mesh['shard'=32,'tensor'=4,'section'=2] {'shard','tensor','section'}, use_global_device_ids=true, to_apply=%region_3.0 | all-reduce | flops 10 | bytes 80 | tf_op jit(solution)/shard_map/psum | solution.py:131
  575.1 1.9 fusion.5
  577.7 7.0 %multiply_add_fusion = f32[3,1024,128]{2,1,0:T(8,128)} fusion(f32[3,1024,128]{2,1,0:T(8,128)} %param.21, bf16[3,1024,1024]{2,1,0:T(8,128)(2,1)} %bitcast.33, s32[]{:T(128)S(6)} %select_n.81), kind=kOutput, calls=%fused_computation.7 | convolution fusion | flops 806486016 | bytes 10223620 | tf_op jit(solution)/shard_map/ski,skj->sij/dot_general | solution.py:115
  584.8 2.9 multiply_add_fusion.1
  587.7 15.3 %all-gather.8.cloned.1.call-done = bf16[32,32,1024]{2,1,0:T(8,128)(2,1)} async-done(((bf16[32,32,128]{2,1,0:T(8,128)(2,1)}), bf16[32,32,1024]{2,1,0:T(8,128)(2,1)}) %all-gather.8.cloned.1.call-update) | async-done | bytes 2097168 | tf_op jit(solution)/shard_map/all_gather | solution.py:155
  603.0 3.2 copy.71
  (65 shorter events, 3.9 us)
Async XLA Ops:
  7.2 66.9 %copy-start = (bf16[32,32,128]{2,1,0:T(8,128)(2,1)S(1)}, bf16[32,32,128]{2,1,0:T(8,128)(2,1)}, u32[]{:S(2)}) copy-start(bf16[32,32,128]{2,1,0:T(8,128)(2,1)} %param.22) | copy-start | bytes 786436
  7.2 63.0 %reduce-scatter.4.cloned.1.call-start = ((), (), s32[]{:S(2)}) async-start(), calls=%async_computation.9 | async-start | bytes 2359296
  19.8 54.0 %copy-start.10 = (s32[32]{0:T(128)S(1)}, s32[32]{0:T(128)}, u32[]{:S(2)}) copy-start(s32[32]{0:T(128)} %param.24) | copy-start | bytes 388
  32.2 70.8 %all-gather.6.cloned.1.call-start = ((), (), s32[]{:S(2)}) async-start(), calls=%async_computation.7 | async-start | bytes 2359296 | tf_op jit(solution)/shard_map/all_gather | solution.py:84
  33.0 102.9 %all-gather.4.cloned.1.call-start = ((), (), s32[]{:S(2)}) async-start(), calls=%async_computation.6 | async-start | bytes 2359296 | tf_op jit(solution)/shard_map/all_gather | solution.py:83
  76.1 78.0 %all-to-all-start = ((bf16[96,32,128]{2,1,0:T(8,128)(2,1)}), bf16[96,32,128]{2,1,0:T(8,128)(2,1)S(1)}, u32[]{:S(2)}, u32[]{:S(2)}) async-start(bf16[96,32,128]{2,1,0:T(8,128)(2,1)} %select_select_fusion.2), calls=%async_computation | async-start | bytes 1572864 | tf_op jit(solution)/shard_map/all_to_all | solution.py:101
  302.8 141.9 %all-to-all-start.2 = ((bf16[96,32,1024]{2,1,0:T(8,128)(2,1)}), bf16[96,32,1024]{2,1,0:T(8,128)(2,1)}, u32[]{:S(2)}, u32[]{:S(2)}) async-start(bf16[96,32,1024]{2,1,0:T(8,128)(2,1)} %get-tuple-element.24), calls=%async_computation.2 | async-start | bytes 12582912 | tf_op jit(solution)/shard_map/all_to_all | solution.py:94
  458.1 36.4 %copy-start.2 = (s32[32]{0:T(128)S(1)}, s32[32]{0:T(128)}, u32[]{:S(2)}) copy-start(s32[32]{0:T(128)} %param.25) | copy-start | bytes 388
  458.1 37.1 %copy-start.3 = (bf16[32,32,128]{2,1,0:T(8,128)(2,1)S(1)}, bf16[32,32,128]{2,1,0:T(8,128)(2,1)}, u32[]{:S(2)}) copy-start(bf16[32,32,128]{2,1,0:T(8,128)(2,1)} %copy.69) | copy-start | bytes 786436
  458.1 37.1 %copy-start.4 = (f32[32,32,128]{2,1,0:T(8,128)S(1)}, f32[32,32,128]{2,1,0:T(8,128)}, u32[]{:S(2)}) copy-start(f32[32,32,128]{2,1,0:T(8,128)} %param.18) | copy-start | bytes 1572868
  458.1 37.1 %copy-start.5 = (f32[32,32,128]{2,1,0:T(8,128)S(1)}, f32[32,32,128]{2,1,0:T(8,128)}, u32[]{:S(2)}) copy-start(f32[32,32,128]{2,1,0:T(8,128)} %param.19) | copy-start | bytes 1572868
  459.5 25.0 %all-to-all-start.3 = ((bf16[3,128,1024]{1,0,2:T(4,128)(2,1)}), bf16[3,128,1024]{1,0,2:T(4,128)(2,1)S(1)}, u32[]{:S(2)}, u32[]{:S(2)}) async-start(bf16[3,128,1024]{1,0,2:T(4,128)(2,1)} %copy.59), calls=%async_computation.3 | async-start | bytes 2097152 | tf_op jit(solution)/shard_map/all_to_all | solution.py:134
  485.0 92.0 %copy-start.6 = (f32[26,256]{1,0:T(8,128)S(1)}, f32[26,256]{1,0:T(8,128)}, u32[]{:S(2)}) copy-start(f32[26,256]{1,0:T(8,128)} %param.26) | copy-start | bytes 79876
  485.0 92.0 %copy-start.7 = (f32[26,256]{1,0:T(8,128)S(1)}, f32[26,256]{1,0:T(8,128)}, u32[]{:S(2)}) copy-start(f32[26,256]{1,0:T(8,128)} %param.28) | copy-start | bytes 79876
  485.1 92.0 %copy-start.8 = (f32[26,256]{1,0:T(8,128)S(1)}, f32[26,256]{1,0:T(8,128)}, u32[]{:S(2)}) copy-start(f32[26,256]{1,0:T(8,128)} %param.29) | copy-start | bytes 79876
  485.1 92.0 %copy-start.9 = (bf16[26,256]{1,0:T(8,128)(2,1)S(1)}, bf16[26,256]{1,0:T(8,128)(2,1)}, u32[]{:S(2)}) copy-start(bf16[26,256]{1,0:T(8,128)(2,1)} %param.27) | copy-start | bytes 39940
  486.7 87.6 %all-to-all-start.4 = ((bf16[3,1024,128]{2,0,1:T(4,128)(2,1)}), bf16[3,1024,128]{2,0,1:T(4,128)(2,1)S(1)}, u32[]{:S(2)}, u32[]{:S(2)}) async-start(bf16[3,1024,128]{2,0,1:T(4,128)(2,1)} %copy.62), calls=%async_computation.4 | async-start | bytes 2097152 | tf_op jit(solution)/shard_map/all_to_all | solution.py:133
  494.3 108.7 %all-gather.8.cloned.1.call-start = ((), (), s32[]{:S(2)}) async-start(), calls=%async_computation.8 | async-start | bytes 2359296 | tf_op jit(solution)/shard_map/all_gather | solution.py:155
  574.4 10.3 %slice-start = ((s8[6291456]{0:T(1024)(128)(4,1)}), s8[2097152]{0:T(1024)(128)(4,1)S(1)}, s32[]{:S(2)}) async-start(s8[6291456]{0:T(1024)(128)(4,1)} %bitcast.34), calls=%async_computation.10 | async-start | bytes 4194304
  577.0 7.7 %copy-start.11 = (f32[3,1024,128]{2,1,0:T(8,128)S(1)}, f32[3,1024,128]{2,1,0:T(8,128)}, u32[]{:S(2)}) copy-start(f32[3,1024,128]{2,1,0:T(8,128)} %param.20) | copy-start | bytes 4718596
  577.7 7.0 %slice-start.1 = ((s8[6291456]{0:T(1024)(128)(4,1)}), s8[4194304]{0:T(1024)(128)(4,1)S(1)}, s32[]{:S(2)}) async-start(s8[6291456]{0:T(1024)(128)(4,1)} %bitcast.34), calls=%async_computation.11 | async-start | bytes 8388608
  577.7 28.5 %copy-start.1 = (bf16[32,32,128]{2,1,0:T(8,128)(2,1)S(1)}, bf16[32,32,128]{2,1,0:T(8,128)(2,1)}, u32[]{:S(2)}) copy-start(bf16[32,32,128]{2,1,0:T(8,128)(2,1)} %param.22) | copy-start | bytes 786436
Sparse Core Ops, SparseCore 0:
  32.3 37.7 reduce-scatter.3
  72.0 31.0 all-gather.5
  105.4 30.4 all-gather.3
  577.1 25.8 all-gather.7
where the time goes:
time: 614 us; the launch traced here: 613 us
  waiting for transfers between devices  240 us (39%)
  blocking collectives  226 us (37%)
  local copies, waits for them, and re-layouts  66.3 us (11%)
  starting transfers between devices  33 us (5%)
  other arithmetic  16.6 us (3%)
  matrix products  16.6 us (3%)
  between operations  14 us (2%)
    all_to_all x1, blocking collectives, shards(): lax.all_to_all(fill_slots(grad_rows, block_ids, occupied), 'shard', split...  149 us
    all_to_all x1, waiting for transfers between devices, shards(): lax.all_to_all(fill_slots(right_rows, block_ids, occupied), 'shard', spli...  129 us
    psum x1, blocking collectives, shards(): lax.psum((adam_part, shampoo_part), ('shard', 'tensor', 'section'))  77.3 us
    unnamed x5, waiting for transfers between devices  37.9 us
    unnamed x33, local copies, waits for them, and re-layouts  31.8 us
    all_gather x1, waiting for transfers between devices, shards(): lax.all_gather(gradient, ('tensor', 'section'), axis=2, tiled=True)  25.4 us
    all_gather x1, waiting for transfers between devices, shards(): lax.all_gather(right_root, ('tensor', 'section'), axis=2, tiled=True)  17.7 us
    gather x3, local copies, waits for them, and re-layouts, fill_slots(): picked = jnp.take(tiles, block_ids, axis=0)  15.8 us
  transfers between devices with their start and end apart: 8, of which 6 were waited for; matrix products, arithmetic and copies ran while one was open for 8% of the time, Pallas kernels for 0%

commit v1 on v0

--- a/solution.py
+++ b/solution.py
@@ -79,67 +79,37 @@
     slot = slot_numbers(block_owner, capacity)
     block_ids, occupied = slot_contents(slot, owners * capacity)
     slab_width = gradient.shape[2]
-    grad_rows, right_rows = (
-        lax.all_gather(gradient, ("tensor", "section"), axis=2, tiled=True),
-        lax.all_gather(right_root, ("tensor", "section"), axis=2, tiled=True),
-    )
-    grad_full, right_full, left_cols = (
-        lax.all_to_all(
-            fill_slots(grad_rows, block_ids, occupied),
-            "shard",
-            split_axis=0,
-            concat_axis=1,
-            tiled=True,
-        ),
-        lax.all_to_all(
-            fill_slots(right_rows, block_ids, occupied),
-            "shard",
-            split_axis=0,
-            concat_axis=1,
-            tiled=True,
-        ),
-        lax.all_to_all(
-            fill_slots(left_root, block_ids, occupied),
-            "shard",
-            split_axis=0,
-            concat_axis=1,
-            tiled=True,
-        ),
-    )
+    def to_block(x):
+        return lax.all_to_all(x, "shard", split_axis=0, concat_axis=1, tiled=True)
+
+    left_cols = to_block(left_root)
+    right_cols = to_block(right_root)
+    left_full = lax.all_gather(left_cols, ("tensor", "section"), axis=2, tiled=True)
+    grad_cols = to_block(gradient)
+    mixed = jnp.einsum(
+        "sij,sjc->sic", left_full, grad_cols, preferred_element_type=jnp.float32
+    ).astype(jnp.bfloat16)
+    mixed_full = lax.all_gather(mixed, ("tensor", "section"), axis=2, tiled=True)
+    precond = jnp.einsum("sik,skc->sic", mixed_full, right_cols, preferred_element_type=jnp.float32)
+    own_matrix = lax.dynamic_slice_in_dim(block_matrix, owner_index, 1)
+    own_onehot = (own_matrix == matrix_range).astype(jnp.float32)
+    shampoo_part = jnp.sum(precond * precond) * own_onehot
+    precond_tile = lax.all_to_all(
+        precond.astype(jnp.bfloat16), "shard", split_axis=1, concat_axis=0, tiled=True
+    ).astype(jnp.float32)
+    slot_cols = to_block(fill_slots(gradient, block_ids, occupied))
+    grad_full = lax.all_gather(slot_cols, ("tensor", "section"), axis=2, tiled=True)
     first_row = group_index * slab_width
     grad_rows_own = lax.dynamic_slice_in_dim(grad_full, first_row, slab_width, 1)
-    grad_cols_own = lax.dynamic_slice_in_dim(grad_full, first_row, slab_width, 2)
     gram_left = jnp.einsum(
         "sik,sjk->sij", grad_full, grad_rows_own, preferred_element_type=jnp.float32
     )
     gram_right = jnp.einsum(
-        "ski,skj->sij", grad_full, grad_cols_own, preferred_element_type=jnp.float32
+        "ski,skj->sij", grad_full, slot_cols, preferred_element_type=jnp.float32
     )
     left_new = BETA_STAT * left_stat + (1.0 - BETA_STAT) * gram_left
     right_new = BETA_STAT * right_stat + (1.0 - BETA_STAT) * gram_right
-    mixed = jnp.einsum(
-        "sjc,sjk->sck", left_cols, grad_full, preferred_element_type=jnp.float32
-    ).astype(jnp.bfloat16)
-    precond = jnp.einsum("sck,skj->scj", mixed, right_full, preferred_element_type=jnp.float32)
-    own_blocks = lax.dynamic_slice_in_dim(block_ids, owner_index * capacity, capacity)
-    own_occupied = lax.dynamic_slice_in_dim(occupied, owner_index * capacity, capacity)
-    own_matrix = jnp.take(block_matrix, own_blocks)
-    slot_onehot = ((own_matrix[:, None] == matrix_range[None, :]) & own_occupied[:, None]).astype(
-        jnp.float32
-    )
-    shampoo_part = jnp.sum(jnp.sum(precond * precond, axis=(1, 2))[:, None] * slot_onehot, axis=0)
     adam_norm, shampoo_norm = lax.psum((adam_part, shampoo_part), ("shard", "tensor", "section"))
-    precond_half = precond.astype(jnp.bfloat16)
-    returned = lax.all_to_all(
-        lax.all_to_all(
-            precond_half, ("tensor", "section"), split_axis=2, concat_axis=1, tiled=True
-        ),
-        "shard",
-        split_axis=1,
-        concat_axis=0,
-        tiled=True,
-    )
-    precond_tile = jnp.take(returned, slot, axis=0).astype(jnp.float32)
     counts = jnp.sum(onehot, axis=0) * float(B * B)
     graft_scale = jnp.sqrt(adam_norm / (shampoo_norm + FLOOR_RATE * counts))
     block_scale = jnp.sum(onehot * graft_scale[None, :], axis=1)

time: 614 us -> 328 us (0.53)
  waiting for transfers between devices: 240 us -> 97 us
  blocking collectives: 226 us -> 127 us
  local copies, waits for them, and re-layouts: 66.3 us -> 35.9 us
  other arithmetic: 16.6 us -> 8.81 us
    all_to_all x4 -> x3, waiting for transfers between devices: 144 us -> 8.76 us  [the longest x2 8.75 us: to_block(): return lax.all_to_all(x, 'shard', split_axis=0, concat_axis=1, tiled=True)]
    all_to_all x1 -> x2, blocking collectives: 149 us -> 50.4 us  [to_block(): return lax.all_to_all(x, 'shard', split_axis=0, concat_axis=1, tiled=True)]
    all_gather x2 -> x3, waiting for transfers between devices: 43 us -> 73.7 us  [the longest x1 44.7 us: shards(): lax.all_gather(slot_cols, ('tensor', 'section'), axis=2, tiled=True)]
    unnamed x5 -> x6, waiting for transfers between devices: 37.9 us -> 14.6 us
    all_gather x1, waiting for transfers between devices: 15.3 us -> 0.01 us  [shards(): lax.all_gather(updated, ('tensor', 'section'), axis=2, tiled=True)]
    all_to_all x8 -> x1, local copies, waits for them, and re-layouts: 15.9 us -> 0.96 us  [to_block(): return lax.all_to_all(x, 'shard', split_axis=0, concat_axis=1, tiled=True)]
    gather x3 -> x1, local copies, waits for them, and re-layouts: 15.8 us -> 1.66 us  [fill_slots(): picked = jnp.take(tiles, block_ids, axis=0)]
    select_n x2 -> x1, other arithmetic: 11.8 us -> 0.27 us  [fill_slots(): return jnp.where(occupied[:, None, None], picked, jnp.zeros_like(picked))]
  transfers between devices with their start and end apart: 8 -> 8, of which waited for: 6 -> 5; matrix products, arithmetic and copies ran while one was open for 8% -> 4% of each run, Pallas kernels for 0% -> 0%
where the time goes in v1:
time: 328 us; the launch traced here: 327 us
  blocking collectives  127 us (39%)
  waiting for transfers between devices  97 us (30%)
  local copies, waits for them, and re-layouts  35.9 us (11%)
  starting transfers between devices  28.4 us (9%)
  matrix products  15.4 us (5%)
  between operations  14 us (4%)
  other arithmetic  8.81 us (3%)
    psum x1, blocking collectives, shards(): lax.psum((adam_part, shampoo_part), ('shard', 'tensor', 'section'))  76.9 us
    all_to_all x2, blocking collectives, to_block(): return lax.all_to_all(x, 'shard', split_axis=0, concat_axis=1, tiled=True)  50.4 us
    all_gather x1, waiting for transfers between devices, shards(): lax.all_gather(slot_cols, ('tensor', 'section'), axis=2, tiled=True)  44.7 us
    unnamed x36, local copies, waits for them, and re-layouts  32.3 us
    all_gather x1, waiting for transfers between devices, shards(): lax.all_gather(left_cols, ('tensor', 'section'), axis=2, tiled=True)  19.8 us
    all_to_all x2, starting transfers between devices, to_block(): return lax.all_to_all(x, 'shard', split_axis=0, concat_axis=1, tiled=True)  18.6 us
    unnamed x6, waiting for transfers between devices  14.6 us
    all_to_all x1, starting transfers between devices, shards(): lax.all_to_all(precond.astype(jnp.bfloat16), 'shard', split_axis=1, conca...  9.54 us
  transfers between devices with their start and end apart: 8, of which 5 were waited for; matrix products, arithmetic and copies ran while one was open for 4% of the time, Pallas kernels for 0%

profile of v1, /device:TPU:1, one launch (start us, length us, event | category | flops | bytes accessed | tf_op | source)
XLA Modules:
  0.0 326.8 jit_solution(6027712454618299210)
XLA Ops:
  7.2 12.5 %copy.31 = bf16[32,32,1024]{1,0,2:T(8,128)(2,1)} copy(bf16[32,32,1024]{2,1,0:T(8,128)(2,1)} %bitcast.39) | data formatting | bytes 4194304
  19.7 12.4 %reshape.91 = bf16[1024,1024]{1,0:T(8,128)(2,1)} reshape(bf16[1024,32,32]{2,1,0:T(8,128)(2,1)} %bitcast.34) | data formatting | bytes 4194304
  32.2 0.9 copy-done.5
  33.1 23.1 %all_to_all.57 = bf16[32,32,128]{2,1,0:T(8,128)(2,1)} all-to-all(bf16[32,32,128]{2,1,0:T(8,128)(2,1)S(1)} %copy-done.5), channel_id=1, replica_groups=mesh['shard'=32,'tensor'=4,'section'=2] {'shard'}, dimensions={0} | all-to-all | bytes 524288 | tf_op jit(solution)/shard_map/all_to_all | solution.py:83
  56.1 14.5 %reduce-scatter.4.cloned.1.call-done = bf16[128,1024]{1,0:T(8,128)(2,1)} async-done(((bf16[1024,1024]{1,0:T(8,128)(2,1)}), bf16[128,1024]{1,0:T(8,128)(2,1)}) %reduce-scatter.4.cloned.1.call-update) | async-done | bytes 262160
  70.6 1.8 reshape.92
  72.5 1.8 copy.32
  74.2 9.1 %all-to-all-start.1 = ((bf16[32,32,128]{2,1,0:T(8,128)(2,1)}), bf16[32,32,128]{2,1,0:T(8,128)(2,1)S(1)}, u32[]{:S(2)}, u32[]{:S(2)}) async-start(bf16[32,32,128]{2,1,0:T(8,128)(2,1)} %copy.32), calls=%async_computation.1 | async-start | bytes 524288 | tf_op jit(solution)/shard_map/all_to_all | solution.py:83
  83.4 19.8 %all-gather.6.cloned.1.call-done = bf16[1,1024,1024]{2,1,0:T(8,128)(2,1)} async-done(((bf16[1,1024,128]{2,1,0:T(8,128)(2,1)}), bf16[1,1024,1024]{2,1,0:T(8,128)(2,1)}) %all-gather.6.cloned.1.call-update) | async-done | bytes 2097168 | tf_op jit(solution)/shard_map/all_gather | solution.py:87
  103.2 3.0 fusion.2
  106.2 9.5 %all-to-all-start.2 = ((bf16[32,32,128]{2,1,0:T(8,128)(2,1)}), bf16[32,32,128]{2,1,0:T(8,128)(2,1)S(1)}, u32[]{:S(2)}, u32[]{:S(2)}) async-start(bf16[32,32,128]{2,1,0:T(8,128)(2,1)} %param.21), calls=%async_computation.2 | async-start | bytes 524288 | tf_op jit(solution)/shard_map/all_to_all | solution.py:83
  115.8 0.6 dynamic_slice.6
  116.4 2.3 multiply_reduce_fusion.1
  118.7 8.8 %all-to-all-done.2 = bf16[32,32,128]{2,1,0:T(8,128)(2,1)S(1)} async-done(((bf16[32,32,128]{2,1,0:T(8,128)(2,1)}), bf16[32,32,128]{2,1,0:T(8,128)(2,1)S(1)}, u32[]{:S(2)}, u32[]{:S(2)}) %all-to-all-start.2) | async-done | bytes 262176 | tf_op jit(solution)/shard_map/all_to_all | solution.py:83
  127.4 9.2 %all-gather.12.cloned.1.call-done = bf16[1024,1024]{1,0:T(8,128)(2,1)} async-done(((bf16[1024,128]{1,0:T(8,128)(2,1)}), bf16[1024,1024]{1,0:T(8,128)(2,1)}) %all-gather.12.cloned.1.call-update) | async-done | bytes 2097168 | tf_op jit(solution)/shard_map/all_gather | solution.py:92
  136.6 2.9 multiply_reduce_fusion
  140.0 0.5 broadcast.81
  140.5 2.2 reduce.2
  142.7 0.8 reshape.93
  143.5 9.5 %all-to-all-start.3 = ((bf16[32,2,2048]{2,1,0:T(2,128)(2,1)}), bf16[32,2,2048]{2,1,0:T(2,128)(2,1)S(1)}, u32[]{:S(2)}, u32[]{:S(2)}) async-start(bf16[32,2,2048]{2,1,0:T(2,128)(2,1)} %reshape.93), calls=%async_computation.3 | async-start | bytes 524288 | tf_op jit(solution)/shard_map/all_to_all | solution.py:97
  153.2 1.3 compare_select_fusion.2
  154.5 76.9 %all-reduce = (f32[5]{0:T(128)S(1)}, f32[5]{0:T(128)S(1)}) all-reduce(f32[5]{0:T(128)S(1)} %get-tuple-element.9, f32[5]{0:T(128)S(1)} %compare_select_fusion.2), channel_id=1, replica_groups=mesh['shard'=32,'tensor'=4,'section'=2] {'shard','tensor','section'}, use_global_device_ids=true, to_apply=%region_3.0 | all-reduce | flops 10 | bytes 80 | tf_op jit(solution)/shard_map/psum | solution.py:112
  231.8 0.5 bitcast_convert_fusion
  232.4 0.9 fusion.8
  233.7 1.7 gather_fusion
  235.7 27.4 %all_to_all.58 = bf16[96,32,128]{2,1,0:T(8,128)(2,1)S(1)} all-to-all(bf16[96,32,128]{2,1,0:T(8,128)(2,1)S(1)} %select_select_fusion), channel_id=1, replica_groups=mesh['shard'=32,'tensor'=4,'section'=2] {'shard'}, dimensions={0} | all-to-all | bytes 1572864 | tf_op jit(solution)/shard_map/all_to_all | solution.py:83
  263.1 1.0 copy.28
  264.1 0.7 multiply_subtract_fusion
  264.8 44.7 %all-gather.10.cloned.1.call-done = bf16[3,1024,1024]{2,1,0:T(8,128)(2,1)} async-done(((bf16[3,1024,128]{2,1,0:T(8,128)(2,1)}), bf16[3,1024,1024]{2,1,0:T(8,128)(2,1)}) %all-gather.10.cloned.1.call-update) | async-done | bytes 6291472 | tf_op jit(solution)/shard_map/all_gather | solution.py:101
  309.5 6.5 %multiply_add_fusion = f32[3,1024,128]{2,1,0:T(8,128)} fusion(f32[3,1024,128]{2,1,0:T(8,128)S(1)} %copy-done.2, bf16[3,1024,1024]{2,1,0:T(8,128)(2,1)} %all-gather.10.cloned.1.call-done, bf16[3,1024,128]{2,1,0:T(8,128)(2,1)} %bitcast.36), kind=kOutput, calls=%fused_computation.3 | convolution fusion | flops 806486016 | bytes 10223616 | tf_op jit(solution)/shard_map/ski,skj->sij/dot_general | solution.py:107
  316.0 2.9 multiply_add_fusion.1
  319.0 1.3 copy.36
  (53 shorter events, 1.9 us)
Async XLA Ops:
  7.2 63.4 %reduce-scatter.4.cloned.1.call-start = ((), (), s32[]{:S(2)}) async-start(), calls=%async_computation.10 | async-start | bytes 2359296
  32.1 0.9 copy-start.5
  32.1 71.0 %all-gather.6.cloned.1.call-start = ((), (), s32[]{:S(2)}) async-start(), calls=%async_computation.6 | async-start | bytes 2359296 | tf_op jit(solution)/shard_map/all_gather | solution.py:87
  74.2 41.5 %copy-start.11 = (s32[32]{0:T(128)S(1)}, s32[32]{0:T(128)}, u32[]{:S(2)}) copy-start(s32[32]{0:T(128)} %param.23) | copy-start | bytes 388
  74.2 42.1 %copy-start.3 = (f32[32,32,128]{2,1,0:T(8,128)S(1)}, f32[32,32,128]{2,1,0:T(8,128)}, u32[]{:S(2)}) copy-start(f32[32,32,128]{2,1,0:T(8,128)} %param.16) | copy-start | bytes 1572868
  74.2 42.1 %copy-start.4 = (f32[32,32,128]{2,1,0:T(8,128)S(1)}, f32[32,32,128]{2,1,0:T(8,128)}, u32[]{:S(2)}) copy-start(f32[32,32,128]{2,1,0:T(8,128)} %param.17) | copy-start | bytes 1572868
  74.2 28.9 %all-to-all-start.1 = ((bf16[32,32,128]{2,1,0:T(8,128)(2,1)}), bf16[32,32,128]{2,1,0:T(8,128)(2,1)S(1)}, u32[]{:S(2)}, u32[]{:S(2)}) async-start(bf16[32,32,128]{2,1,0:T(8,128)(2,1)} %copy.32), calls=%async_computation.1 | async-start | bytes 524288 | tf_op jit(solution)/shard_map/all_to_all | solution.py:83
  83.3 53.3 %all-gather.12.cloned.1.call-start = ((), (), s32[]{:S(2)}) async-start(), calls=%async_computation.9 | async-start | bytes 2359296 | tf_op jit(solution)/shard_map/all_gather | solution.py:92
  106.2 21.2 %all-to-all-start.2 = ((bf16[32,32,128]{2,1,0:T(8,128)(2,1)}), bf16[32,32,128]{2,1,0:T(8,128)(2,1)S(1)}, u32[]{:S(2)}, u32[]{:S(2)}) async-start(bf16[32,32,128]{2,1,0:T(8,128)(2,1)} %param.21), calls=%async_computation.2 | async-start | bytes 524288 | tf_op jit(solution)/shard_map/all_to_all | solution.py:83
  139.5 92.8 %copy-start.6 = (bf16[32,32,128]{2,1,0:T(8,128)(2,1)S(1)}, bf16[32,32,128]{2,1,0:T(8,128)(2,1)}, u32[]{:S(2)}) copy-start(bf16[32,32,128]{2,1,0:T(8,128)(2,1)} %param.15) | copy-start | bytes 786436
  142.7 90.6 %copy-start.13 = (s32[32]{0:T(128)S(1)}, s32[32]{0:T(128)}, u32[]{:S(2)}) copy-start(s32[32]{0:T(128)} %param.22) | copy-start | bytes 388
  143.5 88.0 %all-to-all-start.3 = ((bf16[32,2,2048]{2,1,0:T(2,128)(2,1)}), bf16[32,2,2048]{2,1,0:T(2,128)(2,1)S(1)}, u32[]{:S(2)}, u32[]{:S(2)}) async-start(bf16[32,2,2048]{2,1,0:T(2,128)(2,1)} %reshape.93), calls=%async_computation.3 | async-start | bytes 524288 | tf_op jit(solution)/shard_map/all_to_all | solution.py:97
  153.0 111.8 %all-gather.8.cloned.1.call-start = ((), (), s32[]{:S(2)}) async-start(), calls=%async_computation.7 | async-start | bytes 2359296 | tf_op jit(solution)/shard_map/all_gather | solution.py:125
  233.3 76.2 %all-gather.10.cloned.1.call-start = ((), (), s32[]{:S(2)}) async-start(), calls=%async_computation.8 | async-start | bytes 7077888 | tf_op jit(solution)/shard_map/all_gather | solution.py:101
  235.7 28.4 %copy-start.7 = (f32[26,256]{1,0:T(8,128)S(1)}, f32[26,256]{1,0:T(8,128)}, u32[]{:S(2)}) copy-start(f32[26,256]{1,0:T(8,128)} %param.24) | copy-start | bytes 79876
  235.7 28.4 %copy-start.8 = (f32[26,256]{1,0:T(8,128)S(1)}, f32[26,256]{1,0:T(8,128)}, u32[]{:S(2)}) copy-start(f32[26,256]{1,0:T(8,128)} %param.26) | copy-start | bytes 79876
  235.7 28.4 %copy-start.9 = (f32[26,256]{1,0:T(8,128)S(1)}, f32[26,256]{1,0:T(8,128)}, u32[]{:S(2)}) copy-start(f32[26,256]{1,0:T(8,128)} %param.27) | copy-start | bytes 79876
  235.7 28.4 %copy-start.10 = (bf16[26,256]{1,0:T(8,128)(2,1)S(1)}, bf16[26,256]{1,0:T(8,128)(2,1)}, u32[]{:S(2)}) copy-start(bf16[26,256]{1,0:T(8,128)(2,1)} %param.25) | copy-start | bytes 39940
  235.7 73.7 %copy-start.2 = (f32[3,1024,128]{2,1,0:T(8,128)S(1)}, f32[3,1024,128]{2,1,0:T(8,128)}, u32[]{:S(2)}) copy-start(f32[3,1024,128]{2,1,0:T(8,128)} %param.19) | copy-start | bytes 4718596
  264.8 51.2 %copy-start.12 = (f32[3,1024,128]{2,1,0:T(8,128)S(1)}, f32[3,1024,128]{2,1,0:T(8,128)}, u32[]{:S(2)}) copy-start(f32[3,1024,128]{2,1,0:T(8,128)} %param.18) | copy-start | bytes 4718596
  309.5 6.5 %copy-start = (bf16[3,1024,1024]{2,1,0:T(8,128)(2,1)S(1)}, bf16[3,1024,1024]{2,1,0:T(8,128)(2,1)}, u32[]{:S(2)}) copy-start(bf16[3,1024,1024]{2,1,0:T(8,128)(2,1)} %all-gather.10.cloned.1.call-done) | copy-start | bytes 18874372
  316.0 3.0 copy-start.1
Sparse Core Ops, SparseCore 0:
  32.3 38.3 reduce-scatter.3
  72.4 30.6 all-gather.5
  106.3 30.2 all-gather.11
  233.4 25.8 all-gather.7
  264.2 45.2 all-gather.9

commit v2 on v1

v2 whole, which is shorter than its diff:
```python
import jax
import jax.numpy as jnp
from jax import lax
from jax.experimental import pallas as pl
from jax.experimental.pallas import tpu as pltpu
from jax.sharding import PartitionSpec as P

B = 1024
MATS = 5

BETA_ONE = 0.9
BETA_TWO = 0.95
BETA_STAT = 0.95
LEARNING = 0.1
DECAY_RATE = 0.1
EPSILON = 1e-08
FLOOR_RATE = 1e-06
CORRECT_ONE = 1.0 - 0.9**10
CORRECT_TWO = 1.0 - 0.95**10

MESH = pl.DeviceIdType.MESH
F32 = jnp.float32
BF16 = jnp.bfloat16
OWNERS = 32
RING = 4
GROUP = 8
ROWS = B // OWNERS
WIDTH = B // GROUP
HALF = B // 2
CAP = 3


def adam_direction(grad_float, moment, second):
    moment_new = BETA_ONE * moment + (1.0 - BETA_ONE) * grad_float
    second_new = BETA_TWO * second + (1.0 - BETA_TWO) * grad_float * grad_float
    direction = moment_new / CORRECT_ONE / (jnp.sqrt(second_new / CORRECT_TWO) + EPSILON)
    return (moment_new, second_new, direction)


def slot_numbers(block_owner, capacity):
    positions = jnp.arange(block_owner.shape[0], dtype=jnp.int32)
    earlier = (block_owner[:, None] == block_owner[None, :]) & (
        positions[None, :] < positions[:, None]
    )
    return block_owner * capacity + jnp.sum(earlier.astype(jnp.int32), axis=1)


def slot_contents(slot, slot_total):
    positions = jnp.arange(slot.shape[0], dtype=jnp.int32)
    matches = jnp.arange(slot_total, dtype=jnp.int32)[:, None] == slot[None, :]
    occupied = jnp.any(matches, axis=1)
    block_ids = jnp.sum(jnp.where(matches, positions[None, :], 0), axis=1)
    return (block_ids, occupied)


class Copy:
    def __init__(self, src, dst, send, recv, target, landing=None):
        self.out = pltpu.make_async_remote_copy(
            src_ref=src, dst_ref=dst, send_sem=send, recv_sem=recv, device_id=target,
            device_id_type=MESH,
        )
        here = dst if landing is None else landing
        self.into = pltpu.make_async_remote_copy(
            src_ref=here, dst_ref=here, send_sem=send, recv_sem=recv, device_id=target,
            device_id_type=MESH,
        )

    def start(self):
        self.out.start()

    def wait_recv(self):
        self.into.wait_recv()

    def wait_send(self):
        self.out.wait_send()


def span(start, size):
    return pl.ds(pl.multiple_of(start, size), size)


def kernel(
    ids_ref, parts, weights, adam_m, adam_v, left_stat, right_stat, left_root, right_root,
    mask, same, new_w, m_out, v_out, left_out, right_out,
    mine, pre, ps, rel_a, rel_b, from_minus, from_plus, grad, by_block, packed, left_full, mixed_full,
    new_full, slots, grad_cols, right_cols, pre_half, pre_tile, w_buf, m_buf, v_buf, ls_buf,
    rs_buf, tile_one, norm_one, tile_two, norm_two, sums, scales,
    send_sem, recv_sem, local_sem,
):
    s = lax.axis_index("shard")
    t = lax.axis_index("tensor")
    c = lax.axis_index("section")
    j = t * 2 + c
    up, down, across = lax.rem(t + 1, RING), lax.rem(t + 3, RING), lax.rem(t + 2, RING)
    to_up, to_down = {"tensor": up}, {"tensor": down}
    to_mate = {"section": 1 - c}
    own_cols = span(j * WIDTH, WIDTH)
    own_rows = span(s * ROWS, ROWS)
    counters = {"sem": 0, "local": 0}
    sent = []

    def new_sem():
        index = counters["sem"]
        counters["sem"] += 1
        return send_sem.at[index], recv_sem.at[index]

    def local(src, dst):
        index = counters["local"]
        counters["local"] += 1
        copy = pltpu.make_async_copy(src, dst, local_sem.at[index])
        copy.start()
        return copy

    def remote(src, dst, target, landing=None):
        send, recv = new_sem()
        copy = Copy(src, dst, send, recv, target, landing)
        sent.append(copy)
        return copy

    class Exchange:
        def __init__(self, src, dst, size, fixed=False):
            self.src, self.dst, self.size, self.fixed = src, dst, size, fixed
            self.send, self.recv = new_sem()
            whole = dst(pl.ds(0, (OWNERS - 1) * size))
            self.all = pltpu.make_async_remote_copy(
                src_ref=whole, dst_ref=whole, send_sem=self.send, recv_sem=self.recv,
                device_id={"shard": lax.rem(s + 1, OWNERS)}, device_id_type=MESH,
            )
            sent.append(self)

        def start(self):
            def one(k, carry):
                p = lax.rem(s + k, OWNERS)
                pltpu.make_async_remote_copy(
                    src_ref=self.src(p), dst_ref=self.dst(span(s * self.size, self.size)),
                    send_sem=self.send, recv_sem=self.recv, device_id={"shard": p},
                    device_id_type=MESH,
                ).start()
                return carry

            lax.fori_loop(1, OWNERS, one, 0)

        def wait_recv(self):
            self.all.wait_recv()

        def wait_send(self):
            self.all.wait_send()

    class Gather:
        def __init__(self, full):
            def part(slab, first, size):
                return full.at[pl.ds(first, size), span(slab * WIDTH, WIDTH)]

            own = j
            below, above, far = down * 2 + c, up * 2 + c, across * 2 + c
            lo, hi = (0, HALF), (HALF, HALF)
            self.up_lo = remote(part(own, *lo), part(own, *lo), to_up, part(below, *lo))
            self.up_hi = remote(part(own, *hi), part(own, *hi), to_up, part(below, *hi))
            self.down_hi = remote(part(own, *hi), part(own, *hi), to_down, part(above, *hi))
            self.down_lo = remote(part(own, *lo), part(own, *lo), to_down, part(above, *lo))
            self.fwd_up = remote(part(below, *lo), part(below, *lo), to_up, part(far, *lo))
            self.fwd_down = remote(part(above, *hi), part(above, *hi), to_down, part(far, *hi))
            mates = []
            for row in (t, down, up, across):
                mates.append(
                    remote(
                        part(row * 2 + c, 0, B), part(row * 2 + c, 0, B), to_mate,
                        part(row * 2 + 1 - c, 0, B),
                    )
                )
            self.mates = mates

        def start(self):
            self.up_lo.start()
            self.down_hi.start()
            self.up_hi.start()
            self.down_lo.start()
            self.mates[0].start()

        def relay_one(self):
            self.up_lo.wait_recv()
            self.fwd_up.start()
            self.down_hi.wait_recv()
            self.fwd_down.start()

        def relay_two(self):
            self.up_hi.wait_recv()
            self.mates[1].start()
            self.down_lo.wait_recv()
            self.mates[2].start()

        def relay_three(self):
            self.fwd_up.wait_recv()
            self.fwd_down.wait_recv()
            self.mates[3].start()

        def finish(self):
            for mate in self.mates:
                mate.wait_recv()

    with jax.named_scope("entry"):
        barrier = pltpu.get_barrier_semaphore()

        def greet(k, carry):
            pl.semaphore_signal(
                barrier, inc=1, device_id={"shard": lax.rem(s + k, OWNERS)}, device_id_type=MESH
            )
            return carry

        lax.fori_loop(1, OWNERS, greet, 0)

        def greet_row(q, carry):
            other = lax.rem(j + q, GROUP)
            pl.semaphore_signal(
                barrier, inc=1, device_id={"tensor": other // 2, "section": lax.rem(other, 2)},
                device_id_type=MESH,
            )
            return carry

        lax.fori_loop(1, GROUP, greet_row, 0)

        order = (across, up, down, t)
        mine_in = []
        for slot, row in enumerate(order):
            mine_in.append(
                local(parts.at[:, span((row * 2 + c) * WIDTH, WIDTH)], mine.at[slot])
            )
        right_own = local(right_root.at[own_rows, :], right_cols.at[own_rows, :])
        left_own = local(left_root.at[own_rows, :], left_full.at[own_rows, own_cols])
        m_in = local(adam_m, m_buf)
        v_in = local(adam_v, v_buf)
        w_in = local(weights, w_buf)
        ls_in = local(left_stat, ls_buf)
        rs_in = local(right_stat, rs_buf)
        pl.semaphore_wait(barrier, OWNERS - 1 + GROUP - 1)

    with jax.named_scope("reduce"):
        pairs = []
        for slot, row in enumerate(order):
            pairs.append(
                remote(
                    parts.at[:, span((row * 2 + 1 - c) * WIDTH, WIDTH)], pre.at[slot], to_mate
                )
            )
        for pair in pairs:
            pair.start()
        left_move = Exchange(
            lambda p: left_root.at[span(p * ROWS, ROWS), :],
            lambda rows: left_full.at[rows, own_cols], ROWS,
        )
        right_move = Exchange(
            lambda p: right_root.at[span(p * ROWS, ROWS), :],
            lambda rows: right_cols.at[rows, :], ROWS,
        )
        left_move.start()
        right_move.start()

        lo, hi = pl.ds(0, HALF), pl.ds(HALF, HALF)
        chunk = 64

        def add_up(target, first, rows, terms):
            def one(i, carry):
                at = span(first + i * chunk, chunk)
                total = terms[0](at).astype(F32)
                for term in terms[1:]:
                    total = total + term(at).astype(F32)
                target[at, :] = total.astype(BF16)
                return carry

            lax.fori_loop(0, rows // chunk, one, 0)

        def both(slot):
            mine_in[slot].wait()
            pairs[slot].wait_recv()
            return (lambda at: mine[slot, at, :], lambda at: pre[slot, at, :])

        far_up = remote(ps.at[0, lo, :], rel_a, to_up)
        far_down = remote(ps.at[0, hi, :], rel_b, to_down)
        up_hi = remote(ps.at[1, hi, :], from_minus.at[hi, :], to_up)
        down_lo = remote(ps.at[2, lo, :], from_plus.at[lo, :], to_down)
        up_lo = remote(ps.at[1, lo, :], from_minus.at[lo, :], to_up)
        down_hi = remote(ps.at[2, hi, :], from_plus.at[hi, :], to_down)

        terms = both(0)
        add_up(ps.at[0], 0, B, terms)
        far_up.start()
        far_down.start()
        terms = both(1)
        add_up(ps.at[1], HALF, HALF, terms)
        up_hi.start()
        terms_down = both(2)
        add_up(ps.at[2], 0, HALF, terms_down)
        down_lo.start()
        far_up.wait_recv()
        add_up(ps.at[1], 0, HALF, terms + (lambda at: rel_a[at, :],))
        up_lo.start()
        far_down.wait_recv()
        add_up(
            ps.at[2], HALF, HALF,
            terms_down + (lambda at: rel_b[span(at.start - HALF, chunk), :],),
        )
        down_hi.start()

        left_move.wait_recv()
        left_own.wait()
        left_gather = Gather(left_full)
        left_gather.start()

        terms = both(3)
        for copy in (up_hi, down_lo, up_lo, down_hi):
            copy.wait_recv()
        add_up(
            grad, 0, B, terms + (lambda at: from_minus[at, :], lambda at: from_plus[at, :])
        )

    with jax.named_scope("spread"):
        grad_move = Exchange(
            lambda p: grad.at[span(p * ROWS, ROWS), :], lambda rows: grad_cols.at[rows, :], ROWS
        )
        grad_move.start()
        grad_cols[own_rows, :] = grad[own_rows, :]

        def to_blocks(b, carry):
            by_block[b] = grad[span(b * ROWS, ROWS), :]
            return carry

        lax.fori_loop(0, OWNERS, to_blocks, 0)
        slot_moves = []
        for k in range(CAP):

            def pack(o, carry, k=k):
                q = o * CAP + k
                picked = by_block[ids_ref[q]].astype(F32)
                packed[k, span(o * ROWS, ROWS), :] = (picked * mask[pl.ds(q, 1), :]).astype(BF16)
                return carry

            lax.fori_loop(0, OWNERS, pack, 0)
            move = Exchange(
                lambda p, k=k: packed.at[k, span(p * ROWS, ROWS), :],
                lambda rows, k=k: slots.at[k, rows, own_cols], ROWS,
            )
            move.start()
            slots[k, own_rows, own_cols] = packed[k, own_rows, :]
            slot_moves.append(move)

    left_gather.relay_one()
    with jax.named_scope("moments"):
        m_in.wait()
        v_in.wait()

        def adam(b, carry):
            at = span(b * ROWS, ROWS)
            m_new, v_new, direction = adam_direction(
                grad[at, :].astype(F32), m_buf[at, :], v_buf[at, :]
            )
            m_buf[at, :] = m_new
            v_buf[at, :] = v_new
            sums[pl.ds(b, 1), :] = jnp.sum(direction * direction, axis=0, keepdims=True)
            return carry

        lax.fori_loop(0, OWNERS, adam, 0)
        m_done = local(m_buf, m_out)
        v_done = local(v_buf, v_out)
    left_gather.relay_two()
    left_gather.relay_three()
    left_gather.finish()

    def product(target, lhs, rhs):
        def one(i, carry):
            at = span(i * 256, 256)
            target(
                at, jnp.dot(lhs[at, :], rhs, preferred_element_type=F32)
            )
            return carry

        lax.fori_loop(0, B // 256, one, 0)

    with jax.named_scope("mixed"):
        grad_move.wait_recv()

        def keep_mixed(at, value):
            mixed_full[at, own_cols] = value.astype(BF16)

        product(keep_mixed, left_full, grad_cols[...])
        mixed_gather = Gather(mixed_full)
        mixed_gather.start()
        mixed_gather.relay_one()
    slot_gathers = [Gather(slots.at[k]) for k in range(CAP)]
    slot_moves[0].wait_recv()
    slot_gathers[0].start()
    mixed_gather.relay_two()
    mixed_gather.relay_three()
    slot_gathers[0].relay_one()
    mixed_gather.finish()

    with jax.named_scope("precond"):
        right_move.wait_recv()
        right_own.wait()
        tile_one[...] = jnp.zeros_like(tile_one)
        rhs_right = right_cols[...]

        def one(i, total):
            at = span(i * 256, 256)
            value = jnp.dot(mixed_full[at, :], rhs_right, preferred_element_type=F32)
            pre_half[at, :] = value.astype(BF16)
            return total + jnp.sum(value * value, axis=0, keepdims=True)

        square = lax.fori_loop(0, B // 256, one, jnp.zeros((1, WIDTH), F32))
        norm = jnp.sum(square, axis=1, keepdims=True)
        lane = lax.broadcasted_iota(jnp.int32, (8, 128), 1)
        line = lax.broadcasted_iota(jnp.int32, (8, 128), 0)
        block_sums = jnp.sum(sums[...], axis=1, keepdims=True)
        rows_id = lax.broadcasted_iota(jnp.int32, (OWNERS, 128), 0)
        lanes_id = lax.broadcasted_iota(jnp.int32, (OWNERS, 128), 1)
        adam_row = jnp.sum(jnp.where(rows_id == lanes_id, block_sums, 0.0), axis=0, keepdims=True)
        shampoo_tile = jnp.where((line == 0) & (lane == s), norm, 0.0)
        tile = jnp.where(line == 1, adam_row, shampoo_tile)
        tile_one[...] = tile
        norm_one[span(s * 8, 8), :] = tile
        norm_move = Exchange(lambda p: tile_one, lambda rows: norm_one.at[rows, :], 8)
        norm_move.start()
        back_move = Exchange(
            lambda p: pre_half.at[span(p * ROWS, ROWS), :],
            lambda rows: pre_tile.at[rows, :], ROWS,
        )
        back_move.start()
        pre_tile[own_rows, :] = pre_half[own_rows, :]

    ls_in.wait()
    rs_in.wait()
    stat_done = []

    def grams(k):
        with jax.named_scope("grams"):
            row_block = slots[k, own_cols, :]

            def left(i, carry):
                at = span(i * 256, 256)
                gram = lax.dot_general(
                    slots[k, at, :], row_block, (((1,), (1,)), ((), ())),
                    preferred_element_type=F32,
                )
                ls_buf[k, at, :] = BETA_STAT * ls_buf[k, at, :] + (1.0 - BETA_STAT) * gram
                return carry

            lax.fori_loop(0, B // 256, left, 0)
            stat_done.append(local(ls_buf.at[k], left_out.at[k]))
            flipped = slots[k, :, own_cols].T

            def right(i, carry):
                at = span(i * 256, 256)
                gram = jnp.dot(flipped, slots[k, :, at], preferred_element_type=F32).T
                rs_buf[k, at, :] = BETA_STAT * rs_buf[k, at, :] + (1.0 - BETA_STAT) * gram
                return carry

            lax.fori_loop(0, B // 256, right, 0)
            stat_done.append(local(rs_buf.at[k], right_out.at[k]))

    slot_gathers[0].relay_two()
    slot_moves[1].wait_recv()
    slot_gathers[1].start()
    slot_gathers[0].relay_three()

    with jax.named_scope("norms"):
        norm_move.wait_recv()
        half_sum = jnp.sum(norm_one[...].reshape(OWNERS, 8, 128), axis=0)
        tile_two[...] = half_sum
        norm_two[span(j * 8, 8), :] = half_sum
        send, recv = new_sem()

        def share(q, carry):
            other = lax.rem(j + q, GROUP)
            pltpu.make_async_remote_copy(
                src_ref=tile_two, dst_ref=norm_two.at[span(j * 8, 8), :], send_sem=send,
                recv_sem=recv,
                device_id={"tensor": other // 2, "section": lax.rem(other, 2)},
                device_id_type=MESH,
            ).start()
            return carry

        lax.fori_loop(1, GROUP, share, 0)
        seven = norm_two.at[pl.ds(0, (GROUP - 1) * 8), :]
        shared = Copy(seven, seven, send, recv, to_mate)
        sent.append(shared)

    slot_gathers[1].relay_one()
    slot_gathers[0].finish()
    grams(0)

    with jax.named_scope("update"):
        shared.wait_recv()
        totals = jnp.sum(norm_two[...].reshape(GROUP, 8, 128), axis=0)
        same_value = same[...]
        shampoo = jnp.sum(same_value * totals[0:1, :], axis=1, keepdims=True)
        adam_sum = jnp.sum(same_value * totals[1:2, :], axis=1, keepdims=True)
        counts = jnp.sum(same_value, axis=1, keepdims=True) * float(B * B)
        scale = jnp.sqrt(adam_sum / (shampoo + FLOOR_RATE * counts))
        scales[...] = jnp.broadcast_to(scale, (OWNERS, 128))
        back_move.wait_recv()
        w_in.wait()

        def update(b, carry):
            at = span(b * ROWS, ROWS)
            value = w_buf[at, :].astype(F32)
            step = scales[pl.ds(b, 1), :] * pre_tile[at, :].astype(F32)
            new_full[at, own_cols] = (value - LEARNING * (step + DECAY_RATE * value)).astype(BF16)
            return carry

        lax.fori_loop(0, OWNERS, update, 0)
        new_gather = Gather(new_full)
        new_gather.start()
    slot_gathers[1].relay_two()
    new_gather.relay_one()
    slot_moves[2].wait_recv()
    slot_gathers[2].start()
    slot_gathers[1].relay_three()
    new_gather.relay_two()
    new_gather.relay_three()
    slot_gathers[1].finish()
    slot_gathers[2].relay_one()
    grams(1)
    new_gather.finish()
    new_done = local(new_full, new_w)
    slot_gathers[2].relay_two()
    slot_gathers[2].relay_three()
    slot_gathers[2].finish()
    grams(2)

    for copy in sent:
        copy.wait_send()
    for copy in [m_done, v_done, new_done] + stat_done:
        copy.wait()


def fused_step(ids, parts, weights, m, v, left_stat, right_stat, left_root, right_root, mask, same):
    hbm = pl.BlockSpec(memory_space=pl.ANY)
    vmem = pl.BlockSpec(memory_space=pltpu.VMEM)
    smem = pl.BlockSpec(memory_space=pltpu.SMEM)
    slab = (B, WIDTH)
    full = (B, B)
    return pl.pallas_call(
        kernel,
        out_shape=(
            jax.ShapeDtypeStruct(full, BF16),
            jax.ShapeDtypeStruct(slab, F32),
            jax.ShapeDtypeStruct(slab, F32),
            jax.ShapeDtypeStruct((CAP,) + slab, F32),
            jax.ShapeDtypeStruct((CAP,) + slab, F32),
        ),
        in_specs=[smem] + [hbm] * 8 + [vmem] * 2,
        out_specs=(hbm,) * 5,
        scratch_shapes=[
            pltpu.VMEM((RING,) + slab, BF16),
            pltpu.VMEM((RING,) + slab, BF16),
            pltpu.VMEM((3,) + slab, BF16),
            pltpu.VMEM((HALF, WIDTH), BF16),
            pltpu.VMEM((HALF, WIDTH), BF16),
            pltpu.VMEM(slab, BF16),
            pltpu.VMEM(slab, BF16),
            pltpu.VMEM(slab, BF16),
            pltpu.VMEM((OWNERS, ROWS, WIDTH), BF16),
            pltpu.VMEM((CAP,) + slab, BF16),
            pltpu.VMEM(full, BF16),
            pltpu.VMEM(full, BF16),
            pltpu.VMEM(full, BF16),
            pltpu.VMEM((CAP,) + full, BF16),
            pltpu.VMEM(slab, BF16),
            pltpu.VMEM(slab, BF16),
            pltpu.VMEM(slab, BF16),
            pltpu.VMEM(slab, BF16),
            pltpu.VMEM(slab, BF16),
            pltpu.VMEM(slab, F32),
            pltpu.VMEM(slab, F32),
            pltpu.VMEM((CAP,) + slab, F32),
            pltpu.VMEM((CAP,) + slab, F32),
            pltpu.VMEM((8, 128), F32),
            pltpu.VMEM((OWNERS * 8, 128), F32),
            pltpu.VMEM((8, 128), F32),
            pltpu.VMEM((GROUP * 8, 128), F32),
            pltpu.VMEM((OWNERS, 128), F32),
            pltpu.VMEM((OWNERS, 128), F32),
            pltpu.SemaphoreType.DMA((96,)),
            pltpu.SemaphoreType.DMA((96,)),
            pltpu.SemaphoreType.DMA((32,)),
        ],
        compiler_params=pltpu.CompilerParams(
            collective_id=0, has_side_effects=True, vmem_limit_bytes=56 * 2**20
        ),
        name="shampoo_step",
    )(ids, parts, weights, m, v, left_stat, right_stat, left_root, right_root, mask, same)


def shards(
    grad_parts,
    weights,
    adam_m,
    adam_v,
    left_stat,
    right_stat,
    left_root,
    right_root,
    block_owner,
    block_matrix,
    factors,
    factor_grad,
    factor_m,
    factor_v,
):
    slot = slot_numbers(block_owner, CAP)
    block_ids, occupied = slot_contents(slot, OWNERS * CAP)
    mask = jnp.broadcast_to(occupied.astype(F32)[:, None], (OWNERS * CAP, 128))
    same = jnp.pad(
        (block_matrix[:, None] == block_matrix[None, :]).astype(F32), ((0, 0), (0, 128 - OWNERS))
    )
    new_weights, adam_m_new, adam_v_new, left_new, right_new = fused_step(
        block_ids,
        grad_parts.reshape(B, B),
        weights.reshape(B, WIDTH),
        adam_m.reshape(B, WIDTH),
        adam_v.reshape(B, WIDTH),
        left_stat,
        right_stat,
        left_root.reshape(B, WIDTH),
        right_root.reshape(B, WIDTH),
        mask,
        same,
    )
    factor_m_new, factor_v_new, factor_step = adam_direction(
        factor_grad.astype(F32), factor_m, factor_v
    )
    factors_new = factors - LEARNING * (factor_step + DECAY_RATE * factors)
    return (
        new_weights.reshape(OWNERS, ROWS, B),
        adam_m_new.reshape(OWNERS, ROWS, WIDTH),
        adam_v_new.reshape(OWNERS, ROWS, WIDTH),
        left_new,
        right_new,
        factors_new,
        factor_m_new,
        factor_v_new,
    )


def solution(mesh):
    row = ("tensor", "section")
    slab = P(None, "shard", row)
    stat = P("shard", None, row)
    factor = P("shard", row)
    in_specs = (
        P(row, None, "shard", None), slab, slab, slab, stat, stat, slab, slab, P(), P(),
        factor, factor, factor, factor,
    )
    out_specs = (P(None, "shard", None), slab, slab, stat, stat, factor, factor, factor)
    return jax.shard_map(shards, mesh=mesh, in_specs=in_specs, out_specs=out_specs, check_vma=False)
```

time: 328 us -> 106 us (0.32)
  blocking collectives: 127 us -> 0 us
  waiting for transfers between devices: 97 us -> 0 us
  Pallas kernels: 0 us -> 92.4 us
  starting transfers between devices: 28.4 us -> 0 us
  local copies, waits for them, and re-layouts: 35.9 us -> 8.71 us
  matrix products: 15.4 us -> 0 us
  between operations: 14 us -> 0.69 us
  other arithmetic: 8.81 us -> 4.34 us
    pallas_call x0 -> x1, Pallas kernels: none -> 92.4 us  [fused_step(): pl.pallas_call(kernel, out_shape=(jax.ShapeDtypeStruct(full, BF16), jax.S...]
    psum x1 -> x0, blocking collectives: 76.9 us -> none  [shards(): lax.psum((adam_part, shampoo_part), ('shard', 'tensor', 'section'))]
    all_gather x4 -> x0, waiting for transfers between devices: 73.7 us -> none  [the longest x1 44.7 us: shards(): lax.all_gather(slot_cols, ('tensor', 'section'), axis=2, tiled=True)]
    all_to_all x2 -> x0, blocking collectives: 50.4 us -> none  [to_block(): return lax.all_to_all(x, 'shard', split_axis=0, concat_axis=1, tiled=True)]
    all_to_all x3 -> x0, starting transfers between devices: 28.2 us -> none  [the longest x2 18.6 us: to_block(): return lax.all_to_all(x, 'shard', split_axis=0, concat_axis=1, tiled=True)]
    unnamed x36 -> x21, local copies, waits for them, and re-layouts: 32.3 us -> 8 us
    dot_general x4 -> x0, matrix products: 15.4 us -> none  [the longest x1 6.53 us: shards(): jnp.einsum('ski,skj->sij', grad_full, slot_cols, preferred_element_type=j...]
    unnamed x6 -> x0, waiting for transfers between devices: 14.6 us -> none
  transfers between devices with their start and end apart: 8 -> 0, of which waited for: 5 -> 0; matrix products, arithmetic and copies ran while one was open for 4% -> 0% of each run, Pallas kernels for 0% -> 0%
where the time goes in v2:
time: 106 us
  Pallas kernels  92.4 us (87%)
  local copies, waits for them, and re-layouts  8.71 us (8%)
  other arithmetic  4.34 us (4%)
    pallas_call x1, Pallas kernels, fused_step(): pl.pallas_call(kernel, out_shape=(jax.ShapeDtypeStruct(full, BF16), jax.S...  92.4 us
    unnamed x21, local copies, waits for them, and re-layouts  8 us

profile of v2, /device:TPU:1, one launch (start us, length us, event | category | flops | bytes accessed | tf_op | source)
XLA Modules:
  0.0 106.1 jit_solution(12253033459191557258)
XLA Ops:
  0.6 0.9 convert_reduce_fusion
  1.5 0.7 multiply_add_fusion
  2.2 0.1 fusion.2
  2.3 0.7 broadcast_in_dim.16.mask
  3.0 0.6 select_reduce_fusion.ids_ref
  3.6 0.8 broadcast_compare_fusion
  4.4 0.6 pad_convert_fusion.same
  5.0 0.0 copy-start.4
  5.0 0.0 copy-start.5
  5.0 0.0 copy-start.6
  5.0 0.0 copy-start.7
  5.0 92.4 %shampoo_step.1 = (bf16[1024,1024]{1,0:T(8,128)(2,1)}, f32[1024,128]{1,0:T(8,128)}, f32[1024,128]{1,0:T(8,128)}, f32[3,1024,128]{2,1,0:T(8,128)}, f32[3,1024,128]{2,1,0:T(8,128)}) custom-call(s32[96]{0:T(128)} %select_reduce_fusion.ids_ref, bf16[1024,1024]{1,0:T(8,128)(2,1)} %bitcast.9, bf16[1024,128]{1,0:T(8,128)(2,1)} %bitcast.15, f32[1024,128]{1,0:T(8,128)} %bitcast.11, ...), custom_call_target="tpu_custom_call" | custom-call | tf_op jit(solution)/shard_map/shampoo_step/pallas_call | solution.py:541
  97.4 0.0 copy-done.4
  97.4 0.0 copy-done.5
  97.4 0.0 copy-done.6
  97.4 0.0 copy-done.7
  97.4 0.7 multiply_subtract_fusion
  98.1 0.0 copy-start.3
  98.1 0.0 copy-start.2
  98.1 3.3 %copy.27 = bf16[32,32,1024]{2,1,0:T(8,128)(2,1)} copy(bf16[32,32,1024]{2,1,0:T(8,128)(2,1)} %bitcast.10) | data formatting | bytes 4194304
  101.4 0.0 copy-done.3
  101.4 0.0 copy-start.1
  101.4 0.8 copy.28
  102.2 0.0 copy-done.2
  102.2 0.8 copy.29
  103.0 0.0 copy-done.1
  103.0 0.0 copy-start
  103.0 1.1 %copy.30 = f32[3,1024,128]{2,1,0:T(8,128)} copy(f32[3,1024,128]{2,1,0:T(8,128)S(1)} %copy-done.1) | data formatting | bytes 3145728
  104.1 0.8 copy-done
  105.0 1.1 %copy.31 = f32[3,1024,128]{2,1,0:T(8,128)} copy(f32[3,1024,128]{2,1,0:T(8,128)S(1)} %copy-done) | data formatting | bytes 3145728
  (1 shorter events, 0.0 us)
Async XLA Ops:
  5.0 92.4 %copy-start.4 = (f32[26,256]{1,0:T(8,128)S(1)}, f32[26,256]{1,0:T(8,128)}, u32[]{:S(2)}) copy-start(f32[26,256]{1,0:T(8,128)} %param.24) | copy-start | bytes 79876
  5.0 92.4 %copy-start.5 = (f32[26,256]{1,0:T(8,128)S(1)}, f32[26,256]{1,0:T(8,128)}, u32[]{:S(2)}) copy-start(f32[26,256]{1,0:T(8,128)} %param.26) | copy-start | bytes 79876
  5.0 92.4 %copy-start.6 = (f32[26,256]{1,0:T(8,128)S(1)}, f32[26,256]{1,0:T(8,128)}, u32[]{:S(2)}) copy-start(f32[26,256]{1,0:T(8,128)} %param.27) | copy-start | bytes 79876
  5.0 92.4 %copy-start.7 = (bf16[26,256]{1,0:T(8,128)(2,1)S(1)}, bf16[26,256]{1,0:T(8,128)(2,1)}, u32[]{:S(2)}) copy-start(bf16[26,256]{1,0:T(8,128)(2,1)} %param.25) | copy-start | bytes 39940
  98.1 3.3 %copy-start.3 = (f32[1024,128]{1,0:T(8,128)S(1)}, f32[1024,128]{1,0:T(8,128)}, u32[]{:S(2)}) copy-start(f32[1024,128]{1,0:T(8,128)} %get-tuple-element.14) | copy-start | bytes 1572868
  98.1 4.1 %copy-start.2 = (f32[1024,128]{1,0:T(8,128)S(1)}, f32[1024,128]{1,0:T(8,128)}, u32[]{:S(2)}) copy-start(f32[1024,128]{1,0:T(8,128)} %get-tuple-element.15) | copy-start | bytes 1572868
  101.4 1.6 %copy-start.1 = (f32[3,1024,128]{2,1,0:T(8,128)S(1)}, f32[3,1024,128]{2,1,0:T(8,128)}, u32[]{:S(2)}) copy-start(f32[3,1024,128]{2,1,0:T(8,128)} %get-tuple-element.32) | copy-start | bytes 4718596
  103.0 2.0 %copy-start = (f32[3,1024,128]{2,1,0:T(8,128)S(1)}, f32[3,1024,128]{2,1,0:T(8,128)}, u32[]{:S(2)}) copy-start(f32[3,1024,128]{2,1,0:T(8,128)} %get-tuple-element.33) | copy-start | bytes 4718596

commit v3 on v2

--- a/solution.py
+++ b/solution.py
@@ -28,6 +28,9 @@
 WIDTH = B // GROUP
 HALF = B // 2
 CAP = 3
+NONE = OWNERS
+VMEM_LIMIT = 34 * 2**20
+WRITE_LIMIT = 16 * 2**20
 
 
 def adam_direction(grad_float, moment, second):
@@ -37,20 +40,14 @@
     return (moment_new, second_new, direction)
 
 
-def slot_numbers(block_owner, capacity):
-    positions = jnp.arange(block_owner.shape[0], dtype=jnp.int32)
+def slot_blocks(block_owner):
+    positions = jnp.arange(OWNERS, dtype=jnp.int32)
     earlier = (block_owner[:, None] == block_owner[None, :]) & (
         positions[None, :] < positions[:, None]
     )
-    return block_owner * capacity + jnp.sum(earlier.astype(jnp.int32), axis=1)
-
-
-def slot_contents(slot, slot_total):
-    positions = jnp.arange(slot.shape[0], dtype=jnp.int32)
-    matches = jnp.arange(slot_total, dtype=jnp.int32)[:, None] == slot[None, :]
-    occupied = jnp.any(matches, axis=1)
-    block_ids = jnp.sum(jnp.where(matches, positions[None, :], 0), axis=1)
-    return (block_ids, occupied)
+    slot = block_owner * CAP + jnp.sum(earlier.astype(jnp.int32), axis=1)
+    matches = jnp.arange(OWNERS * CAP, dtype=jnp.int32)[:, None] == slot[None, :]
+    return NONE + jnp.sum(jnp.where(matches, positions[None, :] - NONE, 0), axis=1)
 
 
 class Copy:
@@ -80,11 +77,10 @@
 
 
 def kernel(
-    ids_ref, parts, weights, adam_m, adam_v, left_stat, right_stat, left_root, right_root,
-    mask, same, new_w, m_out, v_out, left_out, right_out,
+    ids_ref, matrix_ref, parts, weights, adam_m, adam_v, left_stat, right_stat, left_root, right_root,
+    new_full, m_buf, v_buf, ls_buf, rs_buf,
     mine, pre, ps, rel_a, rel_b, from_minus, from_plus, grad, by_block, packed, left_full, mixed_full,
-    new_full, slots, grad_cols, right_cols, pre_half, pre_tile, w_buf, m_buf, v_buf, ls_buf,
-    rs_buf, tile_one, norm_one, tile_two, norm_two, sums, scales,
+    slots, grad_cols, right_cols, pre_half, pre_tile, w_buf, tile_one, norm_one, tile_two, norm_two, sums, scales,
     send_sem, recv_sem, local_sem,
 ):
     s = lax.axis_index("shard")
@@ -325,13 +321,13 @@
             return carry
 
         lax.fori_loop(0, OWNERS, to_blocks, 0)
+        by_block[NONE] = jnp.zeros((ROWS, WIDTH), BF16)
         slot_moves = []
         for k in range(CAP):
 
             def pack(o, carry, k=k):
                 q = o * CAP + k
-                picked = by_block[ids_ref[q]].astype(F32)
-                packed[k, span(o * ROWS, ROWS), :] = (picked * mask[pl.ds(q, 1), :]).astype(BF16)
+                packed[k, span(o * ROWS, ROWS), :] = by_block[ids_ref[q]]
                 return carry
 
             lax.fori_loop(0, OWNERS, pack, 0)
@@ -359,8 +355,6 @@
             return carry
 
         lax.fori_loop(0, OWNERS, adam, 0)
-        m_done = local(m_buf, m_out)
-        v_done = local(v_buf, v_out)
     left_gather.relay_two()
     left_gather.relay_three()
     left_gather.finish()
@@ -428,7 +422,6 @@
 
     ls_in.wait()
     rs_in.wait()
-    stat_done = []
 
     def grams(k):
         with jax.named_scope("grams"):
@@ -444,7 +437,6 @@
                 return carry
 
             lax.fori_loop(0, B // 256, left, 0)
-            stat_done.append(local(ls_buf.at[k], left_out.at[k]))
             flipped = slots[k, :, own_cols].T
 
             def right(i, carry):
@@ -454,7 +446,6 @@
                 return carry
 
             lax.fori_loop(0, B // 256, right, 0)
-            stat_done.append(local(rs_buf.at[k], right_out.at[k]))
 
     slot_gathers[0].relay_two()
     slot_moves[1].wait_recv()
@@ -490,7 +481,12 @@
     with jax.named_scope("update"):
         shared.wait_recv()
         totals = jnp.sum(norm_two[...].reshape(GROUP, 8, 128), axis=0)
-        same_value = same[...]
+        names_down = jnp.zeros((OWNERS, 128), jnp.int32)
+        names_along = jnp.full((OWNERS, 128), -1, jnp.int32)
+        for b in range(OWNERS):
+            names_down = jnp.where(rows_id == b, matrix_ref[b], names_down)
+            names_along = jnp.where(lanes_id == b, matrix_ref[b], names_along)
+        same_value = (names_down == names_along).astype(F32)
         shampoo = jnp.sum(same_value * totals[0:1, :], axis=1, keepdims=True)
         adam_sum = jnp.sum(same_value * totals[1:2, :], axis=1, keepdims=True)
         counts = jnp.sum(same_value, axis=1, keepdims=True) * float(B * B)
@@ -520,7 +516,6 @@
     slot_gathers[2].relay_one()
     grams(1)
     new_gather.finish()
-    new_done = local(new_full, new_w)
     slot_gathers[2].relay_two()
     slot_gathers[2].relay_three()
     slot_gathers[2].finish()
@@ -528,27 +523,30 @@
 
     for copy in sent:
         copy.wait_send()
-    for copy in [m_done, v_done, new_done] + stat_done:
-        copy.wait()
-
-
-def fused_step(ids, parts, weights, m, v, left_stat, right_stat, left_root, right_root, mask, same):
-    hbm = pl.BlockSpec(memory_space=pl.ANY)
+
+
+def fused_step(ids, matrix, parts, weights, m, v, left_stat, right_stat, left_root, right_root):
+    hbm = pl.BlockSpec(memory_space=pltpu.HBM)
     vmem = pl.BlockSpec(memory_space=pltpu.VMEM)
     smem = pl.BlockSpec(memory_space=pltpu.SMEM)
     slab = (B, WIDTH)
     full = (B, B)
-    return pl.pallas_call(
+    shapes = (
+        jax.ShapeDtypeStruct(full, BF16),
+        jax.ShapeDtypeStruct(slab, F32),
+        jax.ShapeDtypeStruct(slab, F32),
+        jax.ShapeDtypeStruct((CAP,) + slab, F32),
+        jax.ShapeDtypeStruct((CAP,) + slab, F32),
+    )
+    stay = [
+        pltpu.with_memory_space_constraint(x, pltpu.HBM)
+        for x in (parts, weights, m, v, left_stat, right_stat, left_root, right_root)
+    ]
+    results = pl.pallas_call(
         kernel,
-        out_shape=(
-            jax.ShapeDtypeStruct(full, BF16),
-            jax.ShapeDtypeStruct(slab, F32),
-            jax.ShapeDtypeStruct(slab, F32),
-            jax.ShapeDtypeStruct((CAP,) + slab, F32),
-            jax.ShapeDtypeStruct((CAP,) + slab, F32),
-        ),
-        in_specs=[smem] + [hbm] * 8 + [vmem] * 2,
-        out_specs=(hbm,) * 5,
+        out_shape=tuple(pltpu.VMEM(x.shape, x.dtype) for x in shapes),
+        in_specs=[smem] * 2 + [hbm] * 8,
+        out_specs=(vmem,) * 5,
         scratch_shapes=[
             pltpu.VMEM((RING,) + slab, BF16),
             pltpu.VMEM((RING,) + slab, BF16),
@@ -558,21 +556,16 @@
             pltpu.VMEM(slab, BF16),
             pltpu.VMEM(slab, BF16),
             pltpu.VMEM(slab, BF16),
-            pltpu.VMEM((OWNERS, ROWS, WIDTH), BF16),
+            pltpu.VMEM((OWNERS + 1, ROWS, WIDTH), BF16),
             pltpu.VMEM((CAP,) + slab, BF16),
             pltpu.VMEM(full, BF16),
             pltpu.VMEM(full, BF16),
-            pltpu.VMEM(full, BF16),
             pltpu.VMEM((CAP,) + full, BF16),
             pltpu.VMEM(slab, BF16),
             pltpu.VMEM(slab, BF16),
             pltpu.VMEM(slab, BF16),
             pltpu.VMEM(slab, BF16),
             pltpu.VMEM(slab, BF16),
-            pltpu.VMEM(slab, F32),
-            pltpu.VMEM(slab, F32),
-            pltpu.VMEM((CAP,) + slab, F32),
-            pltpu.VMEM((CAP,) + slab, F32),
             pltpu.VMEM((8, 128), F32),
             pltpu.VMEM((OWNERS * 8, 128), F32),
             pltpu.VMEM((8, 128), F32),
@@ -584,10 +577,30 @@
             pltpu.SemaphoreType.DMA((32,)),
         ],
         compiler_params=pltpu.CompilerParams(
-            collective_id=0, has_side_effects=True, vmem_limit_bytes=56 * 2**20
+            collective_id=0, has_side_effects=True, vmem_limit_bytes=VMEM_LIMIT
         ),
         name="shampoo_step",
-    )(ids, parts, weights, m, v, left_stat, right_stat, left_root, right_root, mask, same)
+    )(ids, matrix, *stay)
+    return pl.pallas_call(
+        write_out,
+        out_shape=shapes,
+        in_specs=[vmem] * 5,
+        out_specs=(hbm,) * 5,
+        scratch_shapes=[pltpu.SemaphoreType.DMA((5,))],
+        compiler_params=pltpu.CompilerParams(vmem_limit_bytes=WRITE_LIMIT),
+        name="write_out",
+    )(*results)
+
+
+def write_out(*refs):
+    copies = [
+        pltpu.make_async_copy(src, dst, refs[10].at[i])
+        for i, (src, dst) in enumerate(zip(refs[:5], refs[5:10]))
+    ]
+    for copy in copies:
+        copy.start()
+    for copy in copies:
+        copy.wait()
 
 
 def shards(
@@ -606,14 +619,10 @@
     factor_m,
     factor_v,
 ):
-    slot = slot_numbers(block_owner, CAP)
-    block_ids, occupied = slot_contents(slot, OWNERS * CAP)
-    mask = jnp.broadcast_to(occupied.astype(F32)[:, None], (OWNERS * CAP, 128))
-    same = jnp.pad(
-        (block_matrix[:, None] == block_matrix[None, :]).astype(F32), ((0, 0), (0, 128 - OWNERS))
-    )
+    block_ids = slot_blocks(block_owner)
     new_weights, adam_m_new, adam_v_new, left_new, right_new = fused_step(
         block_ids,
+        block_matrix,
         grad_parts.reshape(B, B),
         weights.reshape(B, WIDTH),
         adam_m.reshape(B, WIDTH),
@@ -622,8 +631,6 @@
         right_stat,
         left_root.reshape(B, WIDTH),
         right_root.reshape(B, WIDTH),
-        mask,
-        same,
     )
     factor_m_new, factor_v_new, factor_step = adam_direction(
         factor_grad.astype(F32), factor_m, factor_v

time: 106 us -> 98 us (0.925)
  local copies, waits for them, and re-layouts: 8.71 us -> 0.67 us
  other arithmetic: 4.34 us -> 2.33 us
  Pallas kernels: 92.4 us -> 94.2 us
    unnamed x21 -> x10, local copies, waits for them, and re-layouts: 8 us -> 0.67 us
    pallas_call x1 -> x2, Pallas kernels: 92.4 us -> 94.2 us  [the longest x1 91.5 us: fused_step(): pl.pallas_call(kernel, out_shape=tuple((pltpu.VMEM(x.shape, x.dtype) for...]
where the time goes in v3:
time: 98 us; the launch traced here: 97.9 us
  Pallas kernels  94.2 us (96%)
  other arithmetic  2.33 us (2%)
    pallas_call x1, Pallas kernels, fused_step(): pl.pallas_call(kernel, out_shape=tuple((pltpu.VMEM(x.shape, x.dtype) for...  91.5 us
    pallas_call x1, Pallas kernels, fused_step(): pl.pallas_call(write_out, out_shape=shapes, in_specs=[vmem] * 5, out_spec...  2.74 us

profile of v3, /device:TPU:1, one launch (start us, length us, event | category | flops | bytes accessed | tf_op | source)
XLA Modules:
  0.0 97.9 jit_solution(3264260231283109633)
XLA Ops:
  0.6 0.9 convert_reduce_fusion
  1.5 0.7 iota_add_fusion
  2.2 0.1 select_reduce_fusion
  2.3 0.0 copy-start
  2.3 0.6 copy-done
  3.0 91.5 %shampoo_step.1 = (bf16[1024,1024]{1,0:T(8,128)(2,1)S(1)}, f32[1024,128]{1,0:T(8,128)S(1)}, f32[1024,128]{1,0:T(8,128)S(1)}, f32[3,1024,128]{2,1,0:T(8,128)S(1)}, f32[3,1024,128]{2,1,0:T(8,128)S(1)}) custom-call(s32[96]{0:T(128)S(1)} %broadcast_add_fusion.ids_ref, s32[32]{0:T(128)S(1)} %copy-done, bf16[1024,1024]{1,0:T(8,128)(2,1)} %bitcast.9, ...), custom_call_target="tpu_custom_call" | custom-call | tf_op jit(solution)/shard_map/shampoo_step/pallas_call | solution.py:545
  94.4 0.0 copy-start.1
  94.4 0.0 copy-start.2
  94.4 0.0 copy-start.3
  94.5 0.0 copy-start.4
  94.5 2.7 %write_out.1 = (bf16[1024,1024]{1,0:T(8,128)(2,1)}, f32[1024,128]{1,0:T(8,128)}, f32[1024,128]{1,0:T(8,128)}, f32[3,1024,128]{2,1,0:T(8,128)}, f32[3,1024,128]{2,1,0:T(8,128)}) custom-call(bf16[1024,1024]{1,0:T(8,128)(2,1)S(1)} %get-tuple-element.18.refs_0_, f32[1024,128]{1,0:T(8,128)S(1)} %get-tuple-element.19.refs_1_, ...), custom_call_target="tpu_custom_call" | custom-call | tf_op jit(solution)/shard_map/write_out/pallas_call | solution.py:584
  97.2 0.0 copy-done.1
  97.2 0.0 copy-done.2
  97.2 0.0 copy-done.3
  97.3 0.0 copy-done.4
  97.3 0.7 multiply_subtract_fusion
  (1 shorter events, 0.0 us)
Async XLA Ops:
  2.3 0.7 copy-start
  94.4 2.8 %copy-start.1 = (f32[26,256]{1,0:T(8,128)S(1)}, f32[26,256]{1,0:T(8,128)}, u32[]{:S(2)}) copy-start(f32[26,256]{1,0:T(8,128)} %param.24) | copy-start | bytes 79876
  94.4 2.8 %copy-start.2 = (f32[26,256]{1,0:T(8,128)S(1)}, f32[26,256]{1,0:T(8,128)}, u32[]{:S(2)}) copy-start(f32[26,256]{1,0:T(8,128)} %param.26) | copy-start | bytes 79876
  94.4 2.8 %copy-start.3 = (f32[26,256]{1,0:T(8,128)S(1)}, f32[26,256]{1,0:T(8,128)}, u32[]{:S(2)}) copy-start(f32[26,256]{1,0:T(8,128)} %param.27) | copy-start | bytes 79876
  94.5 2.8 %copy-start.4 = (bf16[26,256]{1,0:T(8,128)(2,1)S(1)}, bf16[26,256]{1,0:T(8,128)(2,1)}, u32[]{:S(2)}) copy-start(bf16[26,256]{1,0:T(8,128)(2,1)} %param.25) | copy-start | bytes 39940

commit v4 on v3

--- a/solution.py
+++ b/solution.py
@@ -477,6 +477,10 @@
     slot_gathers[1].relay_one()
     slot_gathers[0].finish()
     grams(0)
+    slot_gathers[1].relay_two()
+    slot_moves[2].wait_recv()
+    slot_gathers[2].start()
+    slot_gathers[1].relay_three()
 
     with jax.named_scope("update"):
         shared.wait_recv()
@@ -505,21 +509,17 @@
         lax.fori_loop(0, OWNERS, update, 0)
         new_gather = Gather(new_full)
         new_gather.start()
-    slot_gathers[1].relay_two()
-    new_gather.relay_one()
-    slot_moves[2].wait_recv()
-    slot_gathers[2].start()
-    slot_gathers[1].relay_three()
-    new_gather.relay_two()
-    new_gather.relay_three()
     slot_gathers[1].finish()
     slot_gathers[2].relay_one()
     grams(1)
-    new_gather.finish()
+    new_gather.relay_one()
     slot_gathers[2].relay_two()
     slot_gathers[2].relay_three()
+    new_gather.relay_two()
+    new_gather.relay_three()
     slot_gathers[2].finish()
     grams(2)
+    new_gather.finish()
 
     for copy in sent:
         copy.wait_send()

time: 98 us -> 93.6 us (0.955)
  Pallas kernels: 94.2 us -> 89.8 us
    pallas_call x1, Pallas kernels: 91.5 us -> 87 us  [fused_step(): pl.pallas_call(kernel, out_shape=tuple((pltpu.VMEM(x.shape, x.dtype) for...]
where the time goes in v4:
time: 93.6 us; the launch traced here: 93.5 us
  Pallas kernels  89.8 us (96%)
  other arithmetic  2.33 us (2%)
    pallas_call x1, Pallas kernels, fused_step(): pl.pallas_call(kernel, out_shape=tuple((pltpu.VMEM(x.shape, x.dtype) for...  87 us
    pallas_call x1, Pallas kernels, fused_step(): pl.pallas_call(write_out, out_shape=shapes, in_specs=[vmem] * 5, out_spec...  2.74 us

profile of v4, /device:TPU:1, one launch (start us, length us, event | category | flops | bytes accessed | tf_op | source)
XLA Modules:
  0.0 93.5 jit_solution(14605293905250907447)
XLA Ops:
  0.6 0.9 convert_reduce_fusion
  1.5 0.7 iota_add_fusion
  2.2 0.1 select_reduce_fusion
  2.3 0.0 copy-start
  2.3 0.6 copy-done
  3.0 87.0 %shampoo_step.1 = (bf16[1024,1024]{1,0:T(8,128)(2,1)S(1)}, f32[1024,128]{1,0:T(8,128)S(1)}, f32[1024,128]{1,0:T(8,128)S(1)}, f32[3,1024,128]{2,1,0:T(8,128)S(1)}, f32[3,1024,128]{2,1,0:T(8,128)S(1)}) custom-call(s32[96]{0:T(128)S(1)} %broadcast_add_fusion.ids_ref, s32[32]{0:T(128)S(1)} %copy-done, bf16[1024,1024]{1,0:T(8,128)(2,1)} %bitcast.9, ...), custom_call_target="tpu_custom_call" | custom-call | tf_op jit(solution)/shard_map/shampoo_step/pallas_call | solution.py:545
  90.0 0.0 copy-start.1
  90.0 0.0 copy-start.2
  90.0 0.0 copy-start.3
  90.0 0.0 copy-start.4
  90.1 2.7 %write_out.1 = (bf16[1024,1024]{1,0:T(8,128)(2,1)}, f32[1024,128]{1,0:T(8,128)}, f32[1024,128]{1,0:T(8,128)}, f32[3,1024,128]{2,1,0:T(8,128)}, f32[3,1024,128]{2,1,0:T(8,128)}) custom-call(bf16[1024,1024]{1,0:T(8,128)(2,1)S(1)} %get-tuple-element.18.refs_0_, f32[1024,128]{1,0:T(8,128)S(1)} %get-tuple-element.19.refs_1_, ...), custom_call_target="tpu_custom_call" | custom-call | tf_op jit(solution)/shard_map/write_out/pallas_call | solution.py:584
  92.8 0.0 copy-done.1
  92.8 0.0 copy-done.2
  92.8 0.0 copy-done.3
  92.8 0.0 copy-done.4
  92.8 0.7 multiply_subtract_fusion
  (1 shorter events, 0.0 us)
Async XLA Ops:
  2.3 0.7 copy-start
  90.0 2.8 %copy-start.1 = (f32[26,256]{1,0:T(8,128)S(1)}, f32[26,256]{1,0:T(8,128)}, u32[]{:S(2)}) copy-start(f32[26,256]{1,0:T(8,128)} %param.24) | copy-start | bytes 79876
  90.0 2.8 %copy-start.2 = (f32[26,256]{1,0:T(8,128)S(1)}, f32[26,256]{1,0:T(8,128)}, u32[]{:S(2)}) copy-start(f32[26,256]{1,0:T(8,128)} %param.26) | copy-start | bytes 79876
  90.0 2.8 %copy-start.3 = (f32[26,256]{1,0:T(8,128)S(1)}, f32[26,256]{1,0:T(8,128)}, u32[]{:S(2)}) copy-start(f32[26,256]{1,0:T(8,128)} %param.27) | copy-start | bytes 79876
  90.0 2.8 %copy-start.4 = (bf16[26,256]{1,0:T(8,128)(2,1)S(1)}, bf16[26,256]{1,0:T(8,128)(2,1)}, u32[]{:S(2)}) copy-start(bf16[26,256]{1,0:T(8,128)(2,1)} %param.25) | copy-start | bytes 39940
